TPU v7x, 32 devices: a whole 2x2x4 slice. The times are simulated.
32 devices in a mesh: dp: 4 (over y, x), pipe: 2 (over core), tensor: 4 (over z).
Axes of the slice: x: 2, y: 2, z: 4, core: 2. Of those that a mesh axis runs over, the one named last changes fastest.
Arguments:
- stream_in: bfloat16 [768, 1536], P('dp'), may hold values from -6 to 6
- segment_ids: int32 [4, 192], P('dp'), may hold values from 0 to 7, never falling along the last dimension, each value on 1 to 96 neighbouring positions
- master_q: float32 [2, 1536, 1536], P('pipe', 'dp', 'tensor')
- moment_q: float32 [2, 1536, 1536], P('pipe', 'dp', 'tensor'), may hold values from -0.046875 to 0.046875
- second_q: float32 [2, 1536, 1536], P('pipe', 'dp', 'tensor'), may hold values from 1e-08 to 1e-06
- grad_q: float32 [2, 1536, 1536], P('pipe', 'dp', 'tensor'), may hold values from -0.15625 to 0.15625
- master_kv: float32 [2, 1536, 512], P('pipe', 'dp', 'tensor')
- moment_kv: float32 [2, 1536, 512], P('pipe', 'dp', 'tensor'), may hold values from -0.046875 to 0.046875
- second_kv: float32 [2, 1536, 512], P('pipe', 'dp', 'tensor'), may hold values from 1e-08 to 1e-06
- grad_kv: float32 [2, 1536, 512], P('pipe', 'dp', 'tensor'), may hold values from -0.15625 to 0.15625
Outputs:
- new_master_q: float32 [2, 1536, 1536], P('pipe', 'dp', 'tensor')
- new_moment_q: float32 [2, 1536, 1536], P('pipe', 'dp', 'tensor')
- new_second_q: float32 [2, 1536, 1536], P('pipe', 'dp', 'tensor')
- new_master_kv: float32 [2, 1536, 512], P('pipe', 'dp', 'tensor')
- new_moment_kv: float32 [2, 1536, 512], P('pipe', 'dp', 'tensor')
- new_second_kv: float32 [2, 1536, 512], P('pipe', 'dp', 'tensor')
- streams_out: bfloat16 [2, 768, 1536], P('pipe', 'dp', 'tensor')
Inputs may be any that keep to these rules, and one draw needn't show every extreme that they name: `segment_ids`: in each row, document numbers never fall and start at 0; every document holds 1 to 96 tokens, one exactly 96.
All inputs are finite; a program needn't handle non-finite values.
Results may differ from a plain program's by a relative error of at most 0.0075.
The roundings to bfloat16 on the way count: a program that leaves them out, or rounds other values in their place, can miss the bound.
Values may be sent and summed in bfloat16 or wider, within the bound.
A program may use at most 64 MiB of HBM per device.

v0:
```python
import functools

import jax
import jax.numpy as jnp
from jax import lax
from jax.experimental import pallas as pl
from jax.experimental.pallas import tpu as pltpu
from jax.sharding import PartitionSpec as P

HEAD_DIM = 128
MESH = pl.DeviceIdType.MESH

beta_one = 0.9
beta_two = 0.999
adam_eps = 1e-08
learn_rate = 0.003
decay_rate = 0.1
adam_step = 10.0
norm_eps = 1e-05


def adamw(master, moment, second, gradient):
    moment_new = beta_one * moment + (1.0 - beta_one) * gradient
    second_new = beta_two * second + (1.0 - beta_two) * gradient * gradient
    fix_one = 1.0 - beta_one**adam_step
    fix_two = 1.0 - beta_two**adam_step
    step_dir = moment_new / fix_one / (jnp.sqrt(second_new / fix_two) + adam_eps)
    master_new = master - learn_rate * (step_dir + decay_rate * master)
    return (master_new, moment_new, second_new)


def write_kernel(*refs):
    count = (len(refs) - 1) // 2
    sems = refs[-1]
    copies = [
        pltpu.make_async_copy(refs[i], refs[count + i], sems.at[i]) for i in range(count)
    ]
    for copy in copies:
        copy.start()
    for copy in copies:
        copy.wait()


def write_call(arrays):
    return pl.pallas_call(
        write_kernel,
        in_specs=[pl.BlockSpec(memory_space=pltpu.VMEM)] * len(arrays),
        out_specs=[pl.BlockSpec(memory_space=pl.ANY)] * len(arrays),
        out_shape=[jax.ShapeDtypeStruct(a.shape, a.dtype) for a in arrays],
        scratch_shapes=[pltpu.SemaphoreType.DMA((len(arrays),))],
    )(*[pltpu.with_memory_space_constraint(a, pltpu.VMEM) for a in arrays])


def sections_kernel(
    n_dp,
    n_tensor,
    x_hbm,
    seg_ref,
    mq_hbm,
    eq_hbm,
    sq_hbm,
    gq_hbm,
    mk_hbm,
    ek_hbm,
    sk_hbm,
    gk_hbm,
    nmq,
    neq,
    nsq,
    nmk,
    nek,
    nsk,
    out_ref,
    x_ref,
    q_ref,
    k_ref,
    load_sem,
    own_ref,
    gathered,
    normed_ref,
    cos_ref,
    sin_ref,
    mask_ref,
    kv_ref,
    first_ref,
    stream_ref,
    send_sem,
    recv_sem,
    own_sem,
    pair_sem,
    stream_send,
    stream_recv,
    go_sem,
):
    dp = lax.axis_index("dp")
    pipe = lax.axis_index("pipe")
    tensor = lax.axis_index("tensor")
    tokens, features = x_ref.shape
    n_pieces, rows, _ = own_ref.shape
    heads = n_pieces - 1
    half = n_tensor // 2
    half_rows = rows // 2
    relayed = n_dp == 4
    holds_key = tensor < half
    pair = lax.rem(tensor + half, n_tensor)
    slot = jnp.where(holds_key, 0, 1)
    f32 = jnp.float32
    bf16 = jnp.bfloat16

    load_x = pltpu.make_async_copy(x_hbm, x_ref, load_sem.at[8])
    loads_k = [
        pltpu.make_async_copy(ref.at[0], k_ref.at[i], load_sem.at[i])
        for i, ref in enumerate((mk_hbm, ek_hbm, sk_hbm, gk_hbm))
    ]
    loads_q = [
        pltpu.make_async_copy(ref.at[0], q_ref.at[i], load_sem.at[4 + i])
        for i, ref in enumerate((mq_hbm, eq_hbm, sq_hbm, gq_hbm))
    ]
    for load in loads_k + loads_q + [load_x]:
        load.start()

    barrier = pltpu.get_barrier_semaphore()
    for off in range(1, n_dp):
        pl.semaphore_signal(
            barrier,
            inc=1,
            device_id=(lax.rem(dp + off, n_dp), pipe, tensor),
            device_id_type=MESH,
        )
    pl.semaphore_signal(barrier, inc=1, device_id=(dp, pipe, pair), device_id_type=MESH)
    for off in range(n_tensor):
        pl.semaphore_signal(
            barrier,
            inc=1,
            device_id=(dp, 1 - pipe, lax.rem(tensor + off, n_tensor)),
            device_id_type=MESH,
        )

    def norm(read_block):
        blocks = features // HEAD_DIM
        squares = jnp.zeros((tokens, HEAD_DIM), f32)
        for b in range(blocks):
            value = read_block(b)
            squares += value * value
        mean = jnp.sum(squares, axis=1, keepdims=True) / features
        scale = lax.rsqrt(mean + norm_eps)
        for b in range(blocks):
            normed_ref[:, b * HEAD_DIM : (b + 1) * HEAD_DIM] = (
                read_block(b) * scale
            ).astype(bf16)

    def tables():
        row = lax.broadcasted_iota(jnp.int32, (tokens, tokens), 0)
        col = lax.broadcasted_iota(jnp.int32, (tokens, tokens), 1)
        seg_row = jnp.broadcast_to(seg_ref[...].astype(f32), (tokens, tokens))
        seg_col = jnp.sum(jnp.where(row == col, seg_row, 0.0), axis=1, keepdims=True)
        same = seg_row == seg_col
        mask_ref[...] = jnp.where(same & (col <= row), 1.0, 0.0)
        position = jnp.sum(jnp.where(same & (col < row), 1.0, 0.0), axis=1, keepdims=True)
        lane = lax.broadcasted_iota(jnp.int32, (1, HEAD_DIM), 1)
        half_dim = HEAD_DIM // 2
        index = jnp.where(lane < half_dim, lane, lane - half_dim).astype(f32)
        inverse_freq = 10000.0 ** (-2.0 * index / HEAD_DIM)
        angles = position * inverse_freq
        cos_ref[...] = jnp.cos(angles)
        sine = jnp.sin(angles)
        sin_ref[...] = jnp.where(lane < half_dim, -sine, sine)

    step_rows = 48 if rows % 48 == 0 else rows

    def update_k(i, carry):
        at = pl.ds(pl.multiple_of(i * step_rows, step_rows), step_rows)
        new = adamw(k_ref[0, at], k_ref[1, at], k_ref[2, at], k_ref[3, at])
        nmk[0, at], nek[0, at], nsk[0, at] = new
        own_ref[0, at] = new[0].astype(bf16)
        return carry

    def update_q(i, carry):
        at = pl.ds(pl.multiple_of(i * step_rows, step_rows), step_rows)
        new = adamw(q_ref[0, at], q_ref[1, at], q_ref[2, at], q_ref[3, at])
        nmq[0, at], neq[0, at], nsq[0, at] = new
        for head in range(heads):
            own_ref[1 + head, at] = new[0][
                :, head * HEAD_DIM : (head + 1) * HEAD_DIM
            ].astype(bf16)
        return carry

    for load in loads_k:
        load.wait()
    lax.fori_loop(0, rows // step_rows, update_k, 0)
    for load in loads_q:
        load.wait()
    lax.fori_loop(0, rows // step_rows, update_q, 0)
    load_x.wait()

    pl.semaphore_wait(barrier, n_dp + n_tensor)

    x_side = dp + 1 - 2 * lax.rem(dp, 2)
    y_side = lax.rem(dp + 2, 4)

    def copy_to(peer, source, target, piece, kind):
        return pltpu.make_async_remote_copy(
            src_ref=source,
            dst_ref=target,
            send_sem=send_sem.at[piece, kind],
            recv_sem=recv_sem.at[piece, kind],
            device_id=(peer, pipe, tensor),
            device_id_type=MESH,
        )

    def own_copies(piece, source):
        target = gathered.at[piece, dp]
        if relayed:
            return [
                copy_to(x_side, source, target, piece, 0),
                copy_to(y_side, source, target, piece, 1),
            ]
        return [
            copy_to(lax.rem(dp + off, n_dp), source, target, piece, off - 1)
            for off in range(1, n_dp)
        ]

    def relay_copies(piece):
        if not relayed:
            return []
        part_a = gathered.at[piece, x_side, pl.ds(0, half_rows)]
        part_b = gathered.at[piece, y_side, pl.ds(half_rows, half_rows)]
        return [
            copy_to(y_side, part_a, part_a, piece, 2),
            copy_to(x_side, part_b, part_b, piece, 3),
        ]

    def start(copies):
        for copy in copies:
            copy.start()

    def relay(piece, source):
        if relayed:
            for copy in own_copies(piece, source):
                copy.wait_recv()
            start(relay_copies(piece))

    def arrived(piece, source):
        copies = relay_copies(piece) if relayed else own_copies(piece, source)
        for copy in copies:
            copy.wait_recv()

    def all_sent(piece, source):
        for copy in own_copies(piece, source) + relay_copies(piece):
            copy.wait_send()

    def keep_own(piece):
        return pltpu.make_async_copy(
            own_ref.at[piece], gathered.at[piece, dp], own_sem.at[piece]
        )

    def weights(piece):
        return gathered[piece].reshape(n_dp * rows, HEAD_DIM)

    def rope(values, cosine, sine):
        return values * cosine + pltpu.roll(values, HEAD_DIM // 2, 1) * sine

    def key_or_value(values, is_key):
        cosine = jnp.where(is_key, cos_ref[...], 1.0)
        sine = jnp.where(is_key, sin_ref[...], 0.0)
        return rope(values, cosine, sine).astype(bf16)

    def attend(head, residual):
        queries = jnp.dot(normed_ref[...], weights(1 + head), preferred_element_type=f32)
        queries = rope(queries, cos_ref[...], sin_ref[...]).astype(bf16)
        scores = lax.dot_general(
            queries, kv_ref[0], (((1,), (1,)), ((), ())), preferred_element_type=f32
        ) * HEAD_DIM ** (-0.5)
        scores = jnp.where(mask_ref[...] > 0.5, scores, -1e30)
        row_max = jnp.max(scores, axis=1, keepdims=True)
        terms = jnp.exp(scores - row_max)
        probs = (terms / jnp.sum(terms, axis=1, keepdims=True)).astype(bf16)
        mixed = jnp.dot(probs, kv_ref[1], preferred_element_type=f32)
        return (residual.astype(f32) + mixed).astype(bf16)

    def pair_block(source, target):
        return pltpu.make_async_remote_copy(
            src_ref=source,
            dst_ref=target,
            send_sem=pair_sem.at[0],
            recv_sem=pair_sem.at[1],
            device_id=(dp, pipe, pair),
            device_id_type=MESH,
        )

    def stream_copy(head, to_tensor):
        return pltpu.make_async_remote_copy(
            src_ref=first_ref.at[head],
            dst_ref=stream_ref.at[tensor * heads + head],
            send_sem=stream_send.at[head, to_tensor],
            recv_sem=stream_recv.at[tensor * heads + head],
            device_id=(dp, 1, to_tensor),
            device_id_type=MESH,
        )

    @pl.when(pipe == 0)
    def _():
        own = [own_ref.at[p] for p in range(n_pieces)]
        ahead = min(3, n_pieces)
        for p in range(ahead):
            start(own_copies(p, own[p]))
        for p in range(n_pieces):
            keep_own(p).start()
        norm(lambda b: x_ref[:, b * HEAD_DIM : (b + 1) * HEAD_DIM].astype(f32))
        tables()
        relay(0, own[0])
        for p in range(ahead, n_pieces):
            start(own_copies(p, own[p]))
        for p in range(1, n_pieces - 1):
            relay(p, own[p])
        for p in range(n_pieces):
            keep_own(p).wait()

        arrived(0, own[0])
        block = jnp.dot(normed_ref[...], weights(0), preferred_element_type=f32)
        kv_ref[slot] = key_or_value(block, holds_key)
        exchange = pair_block(kv_ref.at[slot], kv_ref.at[slot])
        exchange.start()
        relay(n_pieces - 1, own[n_pieces - 1])
        for head in range(heads):
            arrived(1 + head, own[1 + head])
            if head == 0:
                exchange.wait()
                for p in range(n_pieces):
                    all_sent(p, own[p])
                pl.semaphore_signal(
                    go_sem, inc=1, device_id=(dp, 1, tensor), device_id_type=MESH
                )
            columns = pl.ds(
                pl.multiple_of((tensor * heads + head) * HEAD_DIM, HEAD_DIM), HEAD_DIM
            )
            result = attend(head, x_ref[:, columns])
            first_ref[head] = result
            for t in range(n_tensor):
                stream_copy(head, t).start()
            out_ref[:, head * HEAD_DIM : (head + 1) * HEAD_DIM] = result
        for head in range(heads):
            for t in range(n_tensor):
                stream_copy(head, t).wait_send()

    @pl.when(pipe == 1)
    def _():
        own = [own_ref.at[p] for p in range(n_pieces)]
        other = gathered.at[n_pieces, dp]
        exchange = pair_block(own[0], other)
        exchange.start()
        for p in range(n_pieces):
            keep_own(p).start()
        tables()
        for p in range(n_pieces):
            keep_own(p).wait()
        exchange.wait()
        own = own + [other]
        order = [0, n_pieces] + list(range(1, n_pieces))
        pl.semaphore_wait(go_sem, 1)
        ahead = min(3, len(order))
        for p in order[:ahead]:
            start(own_copies(p, own[p]))
        for i, p in enumerate(order):
            relay(p, own[p])
            if i + ahead < len(order):
                q = order[i + ahead]
                start(own_copies(q, own[q]))

        for t in range(n_tensor):
            for head in range(heads):
                pltpu.make_async_remote_copy(
                    src_ref=first_ref.at[head],
                    dst_ref=stream_ref.at[t * heads + head],
                    send_sem=stream_send.at[head, t],
                    recv_sem=stream_recv.at[t * heads + head],
                    device_id=(dp, 0, tensor),
                    device_id_type=MESH,
                ).wait_recv()
        norm(lambda b: stream_ref[b].astype(f32))
        arrived(0, own[0])
        arrived(n_pieces, own[n_pieces])
        block = jnp.dot(normed_ref[...], weights(0), preferred_element_type=f32)
        kv_ref[slot] = key_or_value(block, holds_key)
        block = jnp.dot(normed_ref[...], weights(n_pieces), preferred_element_type=f32)
        kv_ref[1 - slot] = key_or_value(block, jnp.logical_not(holds_key))
        for head in range(heads):
            arrived(1 + head, own[1 + head])
            out_ref[:, head * HEAD_DIM : (head + 1) * HEAD_DIM] = attend(
                head, stream_ref[tensor * heads + head]
            )
        for p in order:
            all_sent(p, own[p])


def sections_call(n_dp, n_tensor, stream, segments, q_arrays, kv_arrays):
    tokens, features = stream.shape
    _, rows, q_cols = q_arrays[0].shape
    kv_cols = kv_arrays[0].shape[2]
    heads = q_cols // HEAD_DIM
    n_pieces = 1 + heads
    kinds = 4 if n_dp == 4 else n_dp - 1
    bf16 = jnp.bfloat16
    f32 = jnp.float32
    vmem = pl.BlockSpec(memory_space=pltpu.VMEM)
    anywhere = pl.BlockSpec(memory_space=pl.ANY)
    return pl.pallas_call(
        functools.partial(sections_kernel, n_dp, n_tensor),
        out_shape=[pltpu.VMEM((1, rows, q_cols), f32)] * 3
        + [pltpu.VMEM((1, rows, kv_cols), f32)] * 3
        + [pltpu.VMEM((tokens, q_cols), bf16)],
        in_specs=[anywhere, vmem] + [anywhere] * 8,
        out_specs=[vmem] * 7,
        scratch_shapes=[
            pltpu.VMEM((tokens, features), bf16),
            pltpu.VMEM((4, rows, q_cols), f32),
            pltpu.VMEM((4, rows, kv_cols), f32),
            pltpu.SemaphoreType.DMA((9,)),
            pltpu.VMEM((n_pieces, rows, HEAD_DIM), bf16),
            pltpu.VMEM((n_pieces + 1, n_dp, rows, HEAD_DIM), bf16),
            pltpu.VMEM((tokens, features), bf16),
            pltpu.VMEM((tokens, HEAD_DIM), jnp.float32),
            pltpu.VMEM((tokens, HEAD_DIM), jnp.float32),
            pltpu.VMEM((tokens, tokens), jnp.float32),
            pltpu.VMEM((2, tokens, HEAD_DIM), bf16),
            pltpu.VMEM((heads, tokens, HEAD_DIM), bf16),
            pltpu.VMEM((n_tensor * heads, tokens, HEAD_DIM), bf16),
            pltpu.SemaphoreType.DMA((n_pieces + 1, kinds)),
            pltpu.SemaphoreType.DMA((n_pieces + 1, kinds)),
            pltpu.SemaphoreType.DMA((n_pieces,)),
            pltpu.SemaphoreType.DMA((2,)),
            pltpu.SemaphoreType.DMA((heads, n_tensor)),
            pltpu.SemaphoreType.DMA((n_tensor * heads,)),
            pltpu.SemaphoreType.REGULAR,
        ],
        compiler_params=pltpu.CompilerParams(collective_id=0, has_side_effects=True),
    )(stream, segments, *q_arrays, *kv_arrays)


def solution(mesh):
    n_dp, n_tensor = mesh.shape["dp"], mesh.shape["tensor"]

    def on_device(
        stream_in,
        segment_ids,
        master_q,
        moment_q,
        second_q,
        grad_q,
        master_kv,
        moment_kv,
        second_kv,
        grad_kv,
    ):
        fresh = sections_call(
            n_dp,
            n_tensor,
            stream_in,
            segment_ids,
            (master_q, moment_q, second_q, grad_q),
            (master_kv, moment_kv, second_kv, grad_kv),
        )
        *states, result = write_call(fresh)
        return (*states, result[None])

    weight_spec = P("pipe", "dp", "tensor")
    return jax.shard_map(
        on_device,
        mesh=mesh,
        in_specs=(P("dp", None), P("dp", None)) + (weight_spec,) * 8,
        out_specs=(weight_spec,) * 7,
        check_vma=False,
    )
```

profile of v0, /device:TPU:1, one launch (start us, length us, event | category | flops | bytes accessed | tf_op | source)
XLA Modules:
  0.0 31.8 jit_solution(8823745715569734557)
XLA Ops:
  0.6 29.7 %shard_map.153 = (f32[1,384,384]{2,1,0:T(8,128)S(1)}, f32[1,384,384]{2,1,0:T(8,128)S(1)}, f32[1,384,384]{2,1,0:T(8,128)S(1)}, f32[1,384,128]{2,1,0:T(8,128)S(1)}...) custom-call(bf16[192,1536]{1,0:T(8,128)(2,1)} %x_hbm.1, s32[1,192]{1,0:T(1,128)} %seg_ref.1, ...), custom_call_target="tpu_custom_call" | custom-call | tf_op jit(solution)/shard_map/pallas_call | solution.py:407
  30.3 1.5 %shard_map.154 = (f32[1,384,384]{2,1,0:T(8,128)}, f32[1,384,384]{2,1,0:T(8,128)}, f32[1,384,384]{2,1,0:T(8,128)}, f32[1,384,128]{2,1,0:T(8,128)}, f32[1,384,128]...) custom-call(f32[1,384,384]{2,1,0:T(8,128)S(1)} %get-tuple-element.21.refs_0_, ...), custom_call_target="tpu_custom_call" | custom-call | tf_op jit(solution)/shard_map/pallas_call | solution.py:45
where the time goes:
time: 32 us; the launch traced here: 31.8 us
  Pallas kernels  31.2 us (98%)
  between operations  0.64 us (2%)
    pallas_call x1, Pallas kernels, sections_call(): pl.pallas_call(functools.partial(sections_kernel, n_dp, n_tensor), out_sh...  29.7 us
    pallas_call x1, Pallas kernels, write_call(): pl.pallas_call(write_kernel, in_specs=[pl.BlockSpec(memory_space=pltpu.VM...  1.5 us

commit v1 on v0

--- a/solution.py
+++ b/solution.py
@@ -55,7 +55,7 @@
     n_dp,
     n_tensor,
     x_hbm,
-    seg_ref,
+    seg_hbm,
     mq_hbm,
     eq_hbm,
     sq_hbm,
@@ -72,21 +72,21 @@
     nsk,
     out_ref,
     x_ref,
+    seg_ref,
     q_ref,
     k_ref,
     load_sem,
-    own_ref,
     gathered,
     normed_ref,
     cos_ref,
     sin_ref,
     mask_ref,
     kv_ref,
+    queries_ref,
     first_ref,
     stream_ref,
     send_sem,
     recv_sem,
-    own_sem,
     pair_sem,
     stream_send,
     stream_recv,
@@ -96,8 +96,9 @@
     pipe = lax.axis_index("pipe")
     tensor = lax.axis_index("tensor")
     tokens, features = x_ref.shape
-    n_pieces, rows, _ = own_ref.shape
-    heads = n_pieces - 1
+    rows = q_ref.shape[1]
+    heads = first_ref.shape[0]
+    n_pieces = 1 + heads
     half = n_tensor // 2
     half_rows = rows // 2
     relayed = n_dp == 4
@@ -107,7 +108,11 @@
     f32 = jnp.float32
     bf16 = jnp.bfloat16
 
+    x_side = dp + 1 - 2 * lax.rem(dp, 2)
+    y_side = lax.rem(dp + 2, 4)
+
     load_x = pltpu.make_async_copy(x_hbm, x_ref, load_sem.at[8])
+    load_seg = pltpu.make_async_copy(seg_hbm, seg_ref, load_sem.at[9])
     loads_k = [
         pltpu.make_async_copy(ref.at[0], k_ref.at[i], load_sem.at[i])
         for i, ref in enumerate((mk_hbm, ek_hbm, sk_hbm, gk_hbm))
@@ -116,16 +121,17 @@
         pltpu.make_async_copy(ref.at[0], q_ref.at[i], load_sem.at[4 + i])
         for i, ref in enumerate((mq_hbm, eq_hbm, sq_hbm, gq_hbm))
     ]
-    for load in loads_k + loads_q + [load_x]:
+    for load in loads_k + loads_q + [load_x, load_seg]:
         load.start()
 
     barrier = pltpu.get_barrier_semaphore()
-    for off in range(1, n_dp):
+    if relayed:
+        near = [x_side, y_side]
+    else:
+        near = [lax.rem(dp + off, n_dp) for off in range(1, n_dp)]
+    for peer in near:
         pl.semaphore_signal(
-            barrier,
-            inc=1,
-            device_id=(lax.rem(dp + off, n_dp), pipe, tensor),
-            device_id_type=MESH,
+            barrier, inc=1, device_id=(peer, pipe, tensor), device_id_type=MESH
         )
     pl.semaphore_signal(barrier, inc=1, device_id=(dp, pipe, pair), device_id_type=MESH)
     for off in range(n_tensor):
@@ -172,87 +178,80 @@
         at = pl.ds(pl.multiple_of(i * step_rows, step_rows), step_rows)
         new = adamw(k_ref[0, at], k_ref[1, at], k_ref[2, at], k_ref[3, at])
         nmk[0, at], nek[0, at], nsk[0, at] = new
-        own_ref[0, at] = new[0].astype(bf16)
+        gathered[0, dp, at] = new[0].astype(bf16)
         return carry
 
-    def update_q(i, carry):
-        at = pl.ds(pl.multiple_of(i * step_rows, step_rows), step_rows)
-        new = adamw(q_ref[0, at], q_ref[1, at], q_ref[2, at], q_ref[3, at])
-        nmq[0, at], neq[0, at], nsq[0, at] = new
-        for head in range(heads):
-            own_ref[1 + head, at] = new[0][
-                :, head * HEAD_DIM : (head + 1) * HEAD_DIM
-            ].astype(bf16)
-        return carry
-
-    for load in loads_k:
-        load.wait()
-    lax.fori_loop(0, rows // step_rows, update_k, 0)
-    for load in loads_q:
-        load.wait()
-    lax.fori_loop(0, rows // step_rows, update_q, 0)
-    load_x.wait()
-
-    pl.semaphore_wait(barrier, n_dp + n_tensor)
-
-    x_side = dp + 1 - 2 * lax.rem(dp, 2)
-    y_side = lax.rem(dp + 2, 4)
-
-    def copy_to(peer, source, target, piece, kind):
+    def update_q(head):
+        columns = slice(head * HEAD_DIM, (head + 1) * HEAD_DIM)
+
+        def step(i, carry):
+            at = pl.ds(pl.multiple_of(i * step_rows, step_rows), step_rows)
+            new = adamw(*[q_ref[n, at, columns] for n in range(4)])
+            nmq[0, at, columns], neq[0, at, columns], nsq[0, at, columns] = new
+            gathered[1 + head, dp, at] = new[0].astype(bf16)
+            return carry
+
+        lax.fori_loop(0, rows // step_rows, step, 0)
+
+    part_a = pl.ds(0, half_rows)
+    part_b = pl.ds(half_rows, half_rows)
+
+    def copy_to(peer, ref, piece, kind):
         return pltpu.make_async_remote_copy(
-            src_ref=source,
-            dst_ref=target,
+            src_ref=ref,
+            dst_ref=ref,
             send_sem=send_sem.at[piece, kind],
             recv_sem=recv_sem.at[piece, kind],
             device_id=(peer, pipe, tensor),
             device_id_type=MESH,
         )
 
-    def own_copies(piece, source):
-        target = gathered.at[piece, dp]
+    def first_copies(piece):
         if relayed:
             return [
-                copy_to(x_side, source, target, piece, 0),
-                copy_to(y_side, source, target, piece, 1),
+                copy_to(x_side, gathered.at[piece, dp, part_a], piece, 0),
+                copy_to(y_side, gathered.at[piece, dp, part_b], piece, 1),
             ]
         return [
-            copy_to(lax.rem(dp + off, n_dp), source, target, piece, off - 1)
+            copy_to(lax.rem(dp + off, n_dp), gathered.at[piece, dp], piece, off - 1)
             for off in range(1, n_dp)
+        ]
+
+    def second_copies(piece):
+        if not relayed:
+            return []
+        return [
+            copy_to(x_side, gathered.at[piece, dp, part_b], piece, 2),
+            copy_to(y_side, gathered.at[piece, dp, part_a], piece, 3),
         ]
 
     def relay_copies(piece):
         if not relayed:
             return []
-        part_a = gathered.at[piece, x_side, pl.ds(0, half_rows)]
-        part_b = gathered.at[piece, y_side, pl.ds(half_rows, half_rows)]
         return [
-            copy_to(y_side, part_a, part_a, piece, 2),
-            copy_to(x_side, part_b, part_b, piece, 3),
+            copy_to(y_side, gathered.at[piece, x_side, part_a], piece, 4),
+            copy_to(x_side, gathered.at[piece, y_side, part_b], piece, 5),
         ]
 
     def start(copies):
         for copy in copies:
             copy.start()
 
-    def relay(piece, source):
-        if relayed:
-            for copy in own_copies(piece, source):
-                copy.wait_recv()
-            start(relay_copies(piece))
-
-    def arrived(piece, source):
-        copies = relay_copies(piece) if relayed else own_copies(piece, source)
-        for copy in copies:
+    def relay(piece):
+        if not relayed:
+            return
+        for got, passed in zip(first_copies(piece), relay_copies(piece)):
+            got.wait_recv()
+            passed.start()
+
+    def arrived(piece):
+        copies = second_copies(piece) + relay_copies(piece)
+        for copy in copies if relayed else first_copies(piece):
             copy.wait_recv()
 
-    def all_sent(piece, source):
-        for copy in own_copies(piece, source) + relay_copies(piece):
+    def all_sent(piece):
+        for copy in first_copies(piece) + second_copies(piece) + relay_copies(piece):
             copy.wait_send()
-
-    def keep_own(piece):
-        return pltpu.make_async_copy(
-            own_ref.at[piece], gathered.at[piece, dp], own_sem.at[piece]
-        )
 
     def weights(piece):
         return gathered[piece].reshape(n_dp * rows, HEAD_DIM)
@@ -265,11 +264,16 @@
         sine = jnp.where(is_key, sin_ref[...], 0.0)
         return rope(values, cosine, sine).astype(bf16)
 
+    def project(head):
+        queries = jnp.dot(normed_ref[...], weights(1 + head), preferred_element_type=f32)
+        queries_ref[head] = rope(queries, cos_ref[...], sin_ref[...]).astype(bf16)
+
     def attend(head, residual):
-        queries = jnp.dot(normed_ref[...], weights(1 + head), preferred_element_type=f32)
-        queries = rope(queries, cos_ref[...], sin_ref[...]).astype(bf16)
         scores = lax.dot_general(
-            queries, kv_ref[0], (((1,), (1,)), ((), ())), preferred_element_type=f32
+            queries_ref[head],
+            kv_ref[0],
+            (((1,), (1,)), ((), ())),
+            preferred_element_type=f32,
         ) * HEAD_DIM ** (-0.5)
         scores = jnp.where(mask_ref[...] > 0.5, scores, -1e30)
         row_max = jnp.max(scores, axis=1, keepdims=True)
@@ -298,39 +302,61 @@
             device_id_type=MESH,
         )
 
+    weight_exchange = pair_block(gathered.at[0, dp], gathered.at[n_pieces, dp])
+
+    for load in loads_k:
+        load.wait()
+    lax.fori_loop(0, rows // step_rows, update_k, 0)
+    pl.semaphore_wait(barrier, len(near) + 1 + n_tensor)
+
     @pl.when(pipe == 0)
     def _():
-        own = [own_ref.at[p] for p in range(n_pieces)]
-        ahead = min(3, n_pieces)
-        for p in range(ahead):
-            start(own_copies(p, own[p]))
-        for p in range(n_pieces):
-            keep_own(p).start()
+        start(first_copies(0) + second_copies(0))
+
+    @pl.when(pipe == 1)
+    def _():
+        weight_exchange.start()
+
+    for load in loads_q:
+        load.wait()
+    update_q(0)
+
+    @pl.when(pipe == 0)
+    def _():
+        start(first_copies(1))
+
+    for head in range(1, heads):
+        update_q(head)
+    load_x.wait()
+    load_seg.wait()
+
+    @pl.when(pipe == 0)
+    def _():
         norm(lambda b: x_ref[:, b * HEAD_DIM : (b + 1) * HEAD_DIM].astype(f32))
         tables()
-        relay(0, own[0])
-        for p in range(ahead, n_pieces):
-            start(own_copies(p, own[p]))
-        for p in range(1, n_pieces - 1):
-            relay(p, own[p])
+        exchange = pair_block(kv_ref.at[slot], kv_ref.at[slot])
         for p in range(n_pieces):
-            keep_own(p).wait()
-
-        arrived(0, own[0])
-        block = jnp.dot(normed_ref[...], weights(0), preferred_element_type=f32)
-        kv_ref[slot] = key_or_value(block, holds_key)
-        exchange = pair_block(kv_ref.at[slot], kv_ref.at[slot])
-        exchange.start()
-        relay(n_pieces - 1, own[n_pieces - 1])
+            relay(p)
+            if p + 1 < n_pieces:
+                start(second_copies(p + 1))
+            if p + 2 < n_pieces:
+                start(first_copies(p + 2))
+            if p == 1:
+                arrived(0)
+                block = jnp.dot(normed_ref[...], weights(0), preferred_element_type=f32)
+                kv_ref[slot] = key_or_value(block, holds_key)
+                exchange.start()
+            if p == 2:
+                arrived(1)
+                project(0)
+        pl.semaphore_signal(
+            go_sem, inc=1, device_id=(dp, 1, tensor), device_id_type=MESH
+        )
+        for head in range(1, heads):
+            arrived(1 + head)
+            project(head)
+        exchange.wait()
         for head in range(heads):
-            arrived(1 + head, own[1 + head])
-            if head == 0:
-                exchange.wait()
-                for p in range(n_pieces):
-                    all_sent(p, own[p])
-                pl.semaphore_signal(
-                    go_sem, inc=1, device_id=(dp, 1, tensor), device_id_type=MESH
-                )
             columns = pl.ds(
                 pl.multiple_of((tensor * heads + head) * HEAD_DIM, HEAD_DIM), HEAD_DIM
             )
@@ -339,33 +365,25 @@
             for t in range(n_tensor):
                 stream_copy(head, t).start()
             out_ref[:, head * HEAD_DIM : (head + 1) * HEAD_DIM] = result
+        for p in range(n_pieces):
+            all_sent(p)
         for head in range(heads):
             for t in range(n_tensor):
                 stream_copy(head, t).wait_send()
 
     @pl.when(pipe == 1)
     def _():
-        own = [own_ref.at[p] for p in range(n_pieces)]
-        other = gathered.at[n_pieces, dp]
-        exchange = pair_block(own[0], other)
-        exchange.start()
-        for p in range(n_pieces):
-            keep_own(p).start()
         tables()
-        for p in range(n_pieces):
-            keep_own(p).wait()
-        exchange.wait()
-        own = own + [other]
+        weight_exchange.wait()
         order = [0, n_pieces] + list(range(1, n_pieces))
         pl.semaphore_wait(go_sem, 1)
-        ahead = min(3, len(order))
-        for p in order[:ahead]:
-            start(own_copies(p, own[p]))
+        start(first_copies(order[0]) + second_copies(order[0]) + first_copies(order[1]))
         for i, p in enumerate(order):
-            relay(p, own[p])
-            if i + ahead < len(order):
-                q = order[i + ahead]
-                start(own_copies(q, own[q]))
+            relay(p)
+            if i + 1 < len(order):
+                start(second_copies(order[i + 1]))
+            if i + 2 < len(order):
+                start(first_copies(order[i + 2]))
 
         for t in range(n_tensor):
             for head in range(heads):
@@ -378,19 +396,20 @@
                     device_id_type=MESH,
                 ).wait_recv()
         norm(lambda b: stream_ref[b].astype(f32))
-        arrived(0, own[0])
-        arrived(n_pieces, own[n_pieces])
+        for p in order:
+            arrived(p)
         block = jnp.dot(normed_ref[...], weights(0), preferred_element_type=f32)
         kv_ref[slot] = key_or_value(block, holds_key)
         block = jnp.dot(normed_ref[...], weights(n_pieces), preferred_element_type=f32)
         kv_ref[1 - slot] = key_or_value(block, jnp.logical_not(holds_key))
         for head in range(heads):
-            arrived(1 + head, own[1 + head])
+            project(head)
+        for head in range(heads):
             out_ref[:, head * HEAD_DIM : (head + 1) * HEAD_DIM] = attend(
                 head, stream_ref[tensor * heads + head]
             )
         for p in order:
-            all_sent(p, own[p])
+            all_sent(p)
 
 
 def sections_call(n_dp, n_tensor, stream, segments, q_arrays, kv_arrays):
@@ -399,7 +418,7 @@
     kv_cols = kv_arrays[0].shape[2]
     heads = q_cols // HEAD_DIM
     n_pieces = 1 + heads
-    kinds = 4 if n_dp == 4 else n_dp - 1
+    kinds = 6 if n_dp == 4 else n_dp - 1
     bf16 = jnp.bfloat16
     f32 = jnp.float32
     vmem = pl.BlockSpec(memory_space=pltpu.VMEM)
@@ -409,14 +428,14 @@
         out_shape=[pltpu.VMEM((1, rows, q_cols), f32)] * 3
         + [pltpu.VMEM((1, rows, kv_cols), f32)] * 3
         + [pltpu.VMEM((tokens, q_cols), bf16)],
-        in_specs=[anywhere, vmem] + [anywhere] * 8,
+        in_specs=[anywhere] * 10,
         out_specs=[vmem] * 7,
         scratch_shapes=[
             pltpu.VMEM((tokens, features), bf16),
+            pltpu.VMEM(segments.shape, jnp.int32),
             pltpu.VMEM((4, rows, q_cols), f32),
             pltpu.VMEM((4, rows, kv_cols), f32),
-            pltpu.SemaphoreType.DMA((9,)),
-            pltpu.VMEM((n_pieces, rows, HEAD_DIM), bf16),
+            pltpu.SemaphoreType.DMA((10,)),
             pltpu.VMEM((n_pieces + 1, n_dp, rows, HEAD_DIM), bf16),
             pltpu.VMEM((tokens, features), bf16),
             pltpu.VMEM((tokens, HEAD_DIM), jnp.float32),
@@ -424,10 +443,10 @@
             pltpu.VMEM((tokens, tokens), jnp.float32),
             pltpu.VMEM((2, tokens, HEAD_DIM), bf16),
             pltpu.VMEM((heads, tokens, HEAD_DIM), bf16),
+            pltpu.VMEM((heads, tokens, HEAD_DIM), bf16),
             pltpu.VMEM((n_tensor * heads, tokens, HEAD_DIM), bf16),
             pltpu.SemaphoreType.DMA((n_pieces + 1, kinds)),
             pltpu.SemaphoreType.DMA((n_pieces + 1, kinds)),
-            pltpu.SemaphoreType.DMA((n_pieces,)),
             pltpu.SemaphoreType.DMA((2,)),
             pltpu.SemaphoreType.DMA((heads, n_tensor)),
             pltpu.SemaphoreType.DMA((n_tensor * heads,)),

time: 32 us -> 31 us (0.969)
  Pallas kernels: 31.2 us -> 30.2 us
    pallas_call x1, Pallas kernels: 29.7 us -> 28.7 us  [sections_call(): pl.pallas_call(functools.partial(sections_kernel, n_dp, n_tensor), out_sh...]
where the time goes in v1:
time: 31 us; the launch traced here: 30.8 us
  Pallas kernels  30.2 us (97%)
  between operations  0.64 us (2%)
    pallas_call x1, Pallas kernels, sections_call(): pl.pallas_call(functools.partial(sections_kernel, n_dp, n_tensor), out_sh...  28.7 us
    pallas_call x1, Pallas kernels, write_call(): pl.pallas_call(write_kernel, in_specs=[pl.BlockSpec(memory_space=pltpu.VM...  1.5 us

profile of v1, /device:TPU:1, one launch (start us, length us, event | category | flops | bytes accessed | tf_op | source)
XLA Modules:
  0.0 30.8 jit_solution(13170844547711316209)
XLA Ops:
  0.6 28.7 %shard_map.153 = (f32[1,384,384]{2,1,0:T(8,128)S(1)}, f32[1,384,384]{2,1,0:T(8,128)S(1)}, f32[1,384,384]{2,1,0:T(8,128)S(1)}, f32[1,384,128]{2,1,0:T(8,128)S(1)}...) custom-call(bf16[192,1536]{1,0:T(8,128)(2,1)} %x_hbm.1, s32[1,192]{1,0:T(1,128)} %seg_hbm.1, ...), custom_call_target="tpu_custom_call" | custom-call | tf_op jit(solution)/shard_map/pallas_call | solution.py:426
  29.3 1.5 %shard_map.154 = (f32[1,384,384]{2,1,0:T(8,128)}, f32[1,384,384]{2,1,0:T(8,128)}, f32[1,384,384]{2,1,0:T(8,128)}, f32[1,384,128]{2,1,0:T(8,128)}, f32[1,384,128]...) custom-call(f32[1,384,384]{2,1,0:T(8,128)S(1)} %get-tuple-element.21.refs_0_, ...), custom_call_target="tpu_custom_call" | custom-call | tf_op jit(solution)/shard_map/pallas_call | solution.py:45

commit v2 on v1

--- a/solution.py
+++ b/solution.py
@@ -83,6 +83,7 @@
     mask_ref,
     kv_ref,
     queries_ref,
+    sums_ref,
     first_ref,
     stream_ref,
     send_sem,
@@ -108,6 +109,18 @@
     f32 = jnp.float32
     bf16 = jnp.bfloat16
 
+    if n_tensor == 4:
+        low = tensor < 2
+        far_first = [
+            jnp.where(low, 3, 0),
+            jnp.where(low, 2, 1),
+            tensor + 1 - 2 * lax.rem(tensor, 2),
+            tensor,
+        ]
+    else:
+        far_first = [lax.rem(tensor + off, n_tensor) for off in range(n_tensor)]
+    blockwise = rows == heads * HEAD_DIM and n_dp == n_tensor
+
     x_side = dp + 1 - 2 * lax.rem(dp, 2)
     y_side = lax.rem(dp + 2, 4)
 
@@ -126,7 +139,7 @@
 
     barrier = pltpu.get_barrier_semaphore()
     if relayed:
-        near = [x_side, y_side]
+        near = [x_side, y_side, 3 - dp]
     else:
         near = [lax.rem(dp + off, n_dp) for off in range(1, n_dp)]
     for peer in near:
@@ -206,28 +219,24 @@
             device_id_type=MESH,
         )
 
-    def first_copies(piece):
+    def direct_copies(piece):
+        own = gathered.at[piece, dp]
         if relayed:
             return [
-                copy_to(x_side, gathered.at[piece, dp, part_a], piece, 0),
-                copy_to(y_side, gathered.at[piece, dp, part_b], piece, 1),
+                copy_to(3 - dp, own, piece, 0),
+                copy_to(x_side, own, piece, 1),
+                copy_to(y_side, own, piece, 2),
             ]
+        return [copy_to(peer, own, piece, n) for n, peer in enumerate(near)]
+
+    def own_copies(piece, kinds=range(4)):
+        peers = (x_side, y_side, x_side, y_side)
+        parts = (part_a, part_b, part_b, part_a)
         return [
-            copy_to(lax.rem(dp + off, n_dp), gathered.at[piece, dp], piece, off - 1)
-            for off in range(1, n_dp)
+            copy_to(peers[n], gathered.at[piece, dp, parts[n]], piece, n) for n in kinds
         ]
 
-    def second_copies(piece):
-        if not relayed:
-            return []
-        return [
-            copy_to(x_side, gathered.at[piece, dp, part_b], piece, 2),
-            copy_to(y_side, gathered.at[piece, dp, part_a], piece, 3),
-        ]
-
     def relay_copies(piece):
-        if not relayed:
-            return []
         return [
             copy_to(y_side, gathered.at[piece, x_side, part_a], piece, 4),
             copy_to(x_side, gathered.at[piece, y_side, part_b], piece, 5),
@@ -237,20 +246,30 @@
         for copy in copies:
             copy.start()
 
+    def send(piece, direct):
+        start(direct_copies(piece) if direct or not relayed else own_copies(piece))
+
     def relay(piece):
         if not relayed:
             return
-        for got, passed in zip(first_copies(piece), relay_copies(piece)):
+        for got, passed in zip(own_copies(piece, (0, 1)), relay_copies(piece)):
             got.wait_recv()
             passed.start()
 
-    def arrived(piece):
-        copies = second_copies(piece) + relay_copies(piece)
-        for copy in copies if relayed else first_copies(piece):
+    def arrived(piece, direct):
+        if direct or not relayed:
+            copies = direct_copies(piece)
+        else:
+            copies = own_copies(piece, (2, 3)) + relay_copies(piece)
+        for copy in copies:
             copy.wait_recv()
 
-    def all_sent(piece):
-        for copy in first_copies(piece) + second_copies(piece) + relay_copies(piece):
+    def all_sent(piece, direct):
+        if direct or not relayed:
+            copies = direct_copies(piece)
+        else:
+            copies = own_copies(piece) + relay_copies(piece)
+        for copy in copies:
             copy.wait_send()
 
     def weights(piece):
@@ -268,19 +287,21 @@
         queries = jnp.dot(normed_ref[...], weights(1 + head), preferred_element_type=f32)
         queries_ref[head] = rope(queries, cos_ref[...], sin_ref[...]).astype(bf16)
 
+    def mix(queries):
+        scores = lax.dot_general(
+            queries, kv_ref[0], (((1,), (1,)), ((), ())), preferred_element_type=f32
+        ) * HEAD_DIM ** (-0.5)
+        scores = scores.reshape(-1, tokens, tokens)
+        scores = jnp.where(mask_ref[...][None] > 0.5, scores, -1e30)
+        row_max = jnp.max(scores, axis=2, keepdims=True)
+        terms = jnp.exp(scores - row_max)
+        probs = (terms / jnp.sum(terms, axis=2, keepdims=True)).astype(bf16)
+        return jnp.dot(
+            probs.reshape(-1, tokens), kv_ref[1], preferred_element_type=f32
+        )
+
     def attend(head, residual):
-        scores = lax.dot_general(
-            queries_ref[head],
-            kv_ref[0],
-            (((1,), (1,)), ((), ())),
-            preferred_element_type=f32,
-        ) * HEAD_DIM ** (-0.5)
-        scores = jnp.where(mask_ref[...] > 0.5, scores, -1e30)
-        row_max = jnp.max(scores, axis=1, keepdims=True)
-        terms = jnp.exp(scores - row_max)
-        probs = (terms / jnp.sum(terms, axis=1, keepdims=True)).astype(bf16)
-        mixed = jnp.dot(probs, kv_ref[1], preferred_element_type=f32)
-        return (residual.astype(f32) + mixed).astype(bf16)
+        return (residual.astype(f32) + mix(queries_ref[head])).astype(bf16)
 
     def pair_block(source, target):
         return pltpu.make_async_remote_copy(
@@ -309,9 +330,11 @@
     lax.fori_loop(0, rows // step_rows, update_k, 0)
     pl.semaphore_wait(barrier, len(near) + 1 + n_tensor)
 
+    direct_pieces = (0, n_pieces - 1)
+
     @pl.when(pipe == 0)
     def _():
-        start(first_copies(0) + second_copies(0))
+        send(0, True)
 
     @pl.when(pipe == 1)
     def _():
@@ -319,14 +342,13 @@
 
     for load in loads_q:
         load.wait()
-    update_q(0)
-
-    @pl.when(pipe == 0)
-    def _():
-        start(first_copies(1))
-
-    for head in range(1, heads):
+    for head in range(heads):
         update_q(head)
+
+        @pl.when(pipe == 0)
+        def _():
+            send(1 + head, 1 + head in direct_pieces)
+
     load_x.wait()
     load_seg.wait()
 
@@ -335,38 +357,32 @@
         norm(lambda b: x_ref[:, b * HEAD_DIM : (b + 1) * HEAD_DIM].astype(f32))
         tables()
         exchange = pair_block(kv_ref.at[slot], kv_ref.at[slot])
-        for p in range(n_pieces):
-            relay(p)
-            if p + 1 < n_pieces:
-                start(second_copies(p + 1))
-            if p + 2 < n_pieces:
-                start(first_copies(p + 2))
-            if p == 1:
-                arrived(0)
-                block = jnp.dot(normed_ref[...], weights(0), preferred_element_type=f32)
-                kv_ref[slot] = key_or_value(block, holds_key)
-                exchange.start()
-            if p == 2:
-                arrived(1)
-                project(0)
+        arrived(0, True)
+        block = jnp.dot(normed_ref[...], weights(0), preferred_element_type=f32)
+        kv_ref[slot] = key_or_value(block, holds_key)
+        exchange.start()
+        for p in range(1, n_pieces):
+            if p not in direct_pieces:
+                relay(p)
         pl.semaphore_signal(
             go_sem, inc=1, device_id=(dp, 1, tensor), device_id_type=MESH
         )
-        for head in range(1, heads):
-            arrived(1 + head)
+        for n in range(heads):
+            head = (n + heads - 1) % heads
+            arrived(1 + head, 1 + head in direct_pieces)
             project(head)
-        exchange.wait()
-        for head in range(heads):
+            if n == 0:
+                exchange.wait()
             columns = pl.ds(
                 pl.multiple_of((tensor * heads + head) * HEAD_DIM, HEAD_DIM), HEAD_DIM
             )
             result = attend(head, x_ref[:, columns])
             first_ref[head] = result
-            for t in range(n_tensor):
+            for t in far_first:
                 stream_copy(head, t).start()
             out_ref[:, head * HEAD_DIM : (head + 1) * HEAD_DIM] = result
         for p in range(n_pieces):
-            all_sent(p)
+            all_sent(p, p in direct_pieces)
         for head in range(heads):
             for t in range(n_tensor):
                 stream_copy(head, t).wait_send()
@@ -377,39 +393,68 @@
         weight_exchange.wait()
         order = [0, n_pieces] + list(range(1, n_pieces))
         pl.semaphore_wait(go_sem, 1)
-        start(first_copies(order[0]) + second_copies(order[0]) + first_copies(order[1]))
-        for i, p in enumerate(order):
+        for p in order:
+            send(p, False)
+        for p in order:
             relay(p)
-            if i + 1 < len(order):
-                start(second_copies(order[i + 1]))
-            if i + 2 < len(order):
-                start(first_copies(order[i + 2]))
-
-        for t in range(n_tensor):
+        for p in order:
+            arrived(p, False)
+
+        def stream_arrived(source):
             for head in range(heads):
                 pltpu.make_async_remote_copy(
                     src_ref=first_ref.at[head],
-                    dst_ref=stream_ref.at[t * heads + head],
-                    send_sem=stream_send.at[head, t],
-                    recv_sem=stream_recv.at[t * heads + head],
+                    dst_ref=stream_ref.at[source * heads + head],
+                    send_sem=stream_send.at[head, source],
+                    recv_sem=stream_recv.at[source * heads + head],
                     device_id=(dp, 0, tensor),
                     device_id_type=MESH,
                 ).wait_recv()
-        norm(lambda b: stream_ref[b].astype(f32))
+
+        if blockwise:
+            squares = jnp.zeros((tokens, HEAD_DIM), f32)
+            for n, source in enumerate(reversed(far_first)):
+                stream_arrived(source)
+                parts = [stream_ref[source * heads + h] for h in range(heads)]
+                for part in parts:
+                    value = part.astype(f32)
+                    squares += value * value
+                block = jnp.dot(
+                    jnp.concatenate(parts, axis=1),
+                    jnp.concatenate([gathered[p, source] for p in order], axis=1),
+                    preferred_element_type=f32,
+                )
+                sums_ref[...] = block if n == 0 else sums_ref[...] + block
+            mean = jnp.sum(squares, axis=1, keepdims=True) / features
+            scale = lax.rsqrt(mean + norm_eps)
+
+            def projected(n):
+                return sums_ref[:, n * HEAD_DIM : (n + 1) * HEAD_DIM] * scale
+
+        else:
+            for source in far_first:
+                stream_arrived(source)
+            norm(lambda b: stream_ref[b].astype(f32))
+
+            def projected(n):
+                return jnp.dot(
+                    normed_ref[...], weights(order[n]), preferred_element_type=f32
+                )
+
+        kv_ref[slot] = key_or_value(projected(0), holds_key)
+        kv_ref[1 - slot] = key_or_value(projected(1), jnp.logical_not(holds_key))
+        queries = [
+            rope(projected(2 + head), cos_ref[...], sin_ref[...]).astype(bf16)
+            for head in range(heads)
+        ]
+        mixed = mix(jnp.concatenate(queries, axis=0))
+        for head in range(heads):
+            residual = stream_ref[tensor * heads + head].astype(f32)
+            out_ref[:, head * HEAD_DIM : (head + 1) * HEAD_DIM] = (
+                residual + mixed[head * tokens : (head + 1) * tokens]
+            ).astype(bf16)
         for p in order:
-            arrived(p)
-        block = jnp.dot(normed_ref[...], weights(0), preferred_element_type=f32)
-        kv_ref[slot] = key_or_value(block, holds_key)
-        block = jnp.dot(normed_ref[...], weights(n_pieces), preferred_element_type=f32)
-        kv_ref[1 - slot] = key_or_value(block, jnp.logical_not(holds_key))
-        for head in range(heads):
-            project(head)
-        for head in range(heads):
-            out_ref[:, head * HEAD_DIM : (head + 1) * HEAD_DIM] = attend(
-                head, stream_ref[tensor * heads + head]
-            )
-        for p in order:
-            all_sent(p)
+            all_sent(p, False)
 
 
 def sections_call(n_dp, n_tensor, stream, segments, q_arrays, kv_arrays):
@@ -443,6 +488,7 @@
             pltpu.VMEM((tokens, tokens), jnp.float32),
             pltpu.VMEM((2, tokens, HEAD_DIM), bf16),
             pltpu.VMEM((heads, tokens, HEAD_DIM), bf16),
+            pltpu.VMEM((tokens, (n_pieces + 1) * HEAD_DIM), f32),
             pltpu.VMEM((heads, tokens, HEAD_DIM), bf16),
             pltpu.VMEM((n_tensor * heads, tokens, HEAD_DIM), bf16),
             pltpu.SemaphoreType.DMA((n_pieces + 1, kinds)),

time: 31 us -> 27.5 us (0.89)
  Pallas kernels: 30.2 us -> 26.7 us
    pallas_call x1, Pallas kernels: 28.7 us -> 25.2 us  [sections_call(): pl.pallas_call(functools.partial(sections_kernel, n_dp, n_tensor), out_sh...]
where the time goes in v2:
time: 27.5 us; the launch traced here: 27.3 us
  Pallas kernels  26.7 us (97%)
  between operations  0.64 us (2%)
    pallas_call x1, Pallas kernels, sections_call(): pl.pallas_call(functools.partial(sections_kernel, n_dp, n_tensor), out_sh...  25.2 us
    pallas_call x1, Pallas kernels, write_call(): pl.pallas_call(write_kernel, in_specs=[pl.BlockSpec(memory_space=pltpu.VM...  1.5 us

profile of v2, /device:TPU:1, one launch (start us, length us, event | category | flops | bytes accessed | tf_op | source)
XLA Modules:
  0.0 27.3 jit_solution(17329857500072487834)
XLA Ops:
  0.6 25.2 %shard_map.153 = (f32[1,384,384]{2,1,0:T(8,128)S(1)}, f32[1,384,384]{2,1,0:T(8,128)S(1)}, f32[1,384,384]{2,1,0:T(8,128)S(1)}, f32[1,384,128]{2,1,0:T(8,128)S(1)}...) custom-call(bf16[192,1536]{1,0:T(8,128)(2,1)} %x_hbm.1, s32[1,192]{1,0:T(1,128)} %seg_hbm.1, ...), custom_call_target="tpu_custom_call" | custom-call | tf_op jit(solution)/shard_map/pallas_call | solution.py:471
  25.8 1.5 %shard_map.154 = (f32[1,384,384]{2,1,0:T(8,128)}, f32[1,384,384]{2,1,0:T(8,128)}, f32[1,384,384]{2,1,0:T(8,128)}, f32[1,384,128]{2,1,0:T(8,128)}, f32[1,384,128]...) custom-call(f32[1,384,384]{2,1,0:T(8,128)S(1)} %get-tuple-element.21.refs_0_, ...), custom_call_target="tpu_custom_call" | custom-call | tf_op jit(solution)/shard_map/pallas_call | solution.py:45

commit v3 on v2

--- a/solution.py
+++ b/solution.py
@@ -32,9 +32,16 @@
 def write_kernel(*refs):
     count = (len(refs) - 1) // 2
     sems = refs[-1]
-    copies = [
-        pltpu.make_async_copy(refs[i], refs[count + i], sems.at[i]) for i in range(count)
-    ]
+    copies = []
+    for i in range(count):
+        source, target = refs[i], refs[count + i]
+        rows = source.shape[-2]
+        step = rows // 3 if rows % 24 == 0 and source.dtype == jnp.float32 else rows
+        for n in range(rows // step):
+            at = (Ellipsis, pl.ds(n * step, step), slice(None))
+            copies.append(
+                pltpu.make_async_copy(source.at[at], target.at[at], sems.at[i, n])
+            )
     for copy in copies:
         copy.start()
     for copy in copies:
@@ -47,7 +54,7 @@
         in_specs=[pl.BlockSpec(memory_space=pltpu.VMEM)] * len(arrays),
         out_specs=[pl.BlockSpec(memory_space=pl.ANY)] * len(arrays),
         out_shape=[jax.ShapeDtypeStruct(a.shape, a.dtype) for a in arrays],
-        scratch_shapes=[pltpu.SemaphoreType.DMA((len(arrays),))],
+        scratch_shapes=[pltpu.SemaphoreType.DMA((len(arrays), 3))],
     )(*[pltpu.with_memory_space_constraint(a, pltpu.VMEM) for a in arrays])
 
 
@@ -100,29 +107,38 @@
     rows = q_ref.shape[1]
     heads = first_ref.shape[0]
     n_pieces = 1 + heads
-    half = n_tensor // 2
     half_rows = rows // 2
     relayed = n_dp == 4
+    half = n_tensor // 2
+    pair = lax.rem(tensor + half, n_tensor)
     holds_key = tensor < half
-    pair = lax.rem(tensor + half, n_tensor)
     slot = jnp.where(holds_key, 0, 1)
     f32 = jnp.float32
     bf16 = jnp.bfloat16
 
     if n_tensor == 4:
-        low = tensor < 2
-        far_first = [
-            jnp.where(low, 3, 0),
-            jnp.where(low, 2, 1),
-            tensor + 1 - 2 * lax.rem(tensor, 2),
-            tensor,
-        ]
+        far_first = [3 - tensor, pair, tensor + 1 - 2 * lax.rem(tensor, 2), tensor]
     else:
         far_first = [lax.rem(tensor + off, n_tensor) for off in range(n_tensor)]
     blockwise = rows == heads * HEAD_DIM and n_dp == n_tensor
 
     x_side = dp + 1 - 2 * lax.rem(dp, 2)
     y_side = lax.rem(dp + 2, 4)
+
+    barrier = pltpu.get_barrier_semaphore()
+    if relayed:
+        near = [x_side, y_side, 3 - dp]
+    else:
+        near = [lax.rem(dp + off, n_dp) for off in range(1, n_dp)]
+    for peer in near:
+        pl.semaphore_signal(
+            barrier, inc=1, device_id=(peer, pipe, tensor), device_id_type=MESH
+        )
+    pl.semaphore_signal(barrier, inc=1, device_id=(dp, pipe, pair), device_id_type=MESH)
+    for t in far_first[1:] if n_tensor == 4 else far_first:
+        pl.semaphore_signal(
+            barrier, inc=1, device_id=(dp, 1 - pipe, t), device_id_type=MESH
+        )
 
     load_x = pltpu.make_async_copy(x_hbm, x_ref, load_sem.at[8])
     load_seg = pltpu.make_async_copy(seg_hbm, seg_ref, load_sem.at[9])
@@ -136,24 +152,6 @@
     ]
     for load in loads_k + loads_q + [load_x, load_seg]:
         load.start()
-
-    barrier = pltpu.get_barrier_semaphore()
-    if relayed:
-        near = [x_side, y_side, 3 - dp]
-    else:
-        near = [lax.rem(dp + off, n_dp) for off in range(1, n_dp)]
-    for peer in near:
-        pl.semaphore_signal(
-            barrier, inc=1, device_id=(peer, pipe, tensor), device_id_type=MESH
-        )
-    pl.semaphore_signal(barrier, inc=1, device_id=(dp, pipe, pair), device_id_type=MESH)
-    for off in range(n_tensor):
-        pl.semaphore_signal(
-            barrier,
-            inc=1,
-            device_id=(dp, 1 - pipe, lax.rem(tensor + off, n_tensor)),
-            device_id_type=MESH,
-        )
 
     def norm(read_block):
         blocks = features // HEAD_DIM
@@ -328,9 +326,9 @@
     for load in loads_k:
         load.wait()
     lax.fori_loop(0, rows // step_rows, update_k, 0)
-    pl.semaphore_wait(barrier, len(near) + 1 + n_tensor)
-
-    direct_pieces = (0, n_pieces - 1)
+    pl.semaphore_wait(barrier, len(near) + 1 + n_tensor - (n_tensor == 4))
+
+    direct_pieces = (0, 1)
 
     @pl.when(pipe == 0)
     def _():
@@ -361,17 +359,15 @@
         block = jnp.dot(normed_ref[...], weights(0), preferred_element_type=f32)
         kv_ref[slot] = key_or_value(block, holds_key)
         exchange.start()
-        for p in range(1, n_pieces):
-            if p not in direct_pieces:
-                relay(p)
         pl.semaphore_signal(
             go_sem, inc=1, device_id=(dp, 1, tensor), device_id_type=MESH
         )
-        for n in range(heads):
-            head = (n + heads - 1) % heads
+        for head in range(heads):
             arrived(1 + head, 1 + head in direct_pieces)
             project(head)
-            if n == 0:
+            if head == 0:
+                for p in range(2, n_pieces):
+                    relay(p)
                 exchange.wait()
             columns = pl.ds(
                 pl.multiple_of((tensor * heads + head) * HEAD_DIM, HEAD_DIM), HEAD_DIM
@@ -397,7 +393,7 @@
             send(p, False)
         for p in order:
             relay(p)
-        for p in order:
+        for p in order[:-1] if blockwise else order:
             arrived(p, False)
 
         def stream_arrived(source):
@@ -412,19 +408,44 @@
                 ).wait_recv()
 
         if blockwise:
-            squares = jnp.zeros((tokens, HEAD_DIM), f32)
-            for n, source in enumerate(reversed(far_first)):
-                stream_arrived(source)
-                parts = [stream_ref[source * heads + h] for h in range(heads)]
-                for part in parts:
-                    value = part.astype(f32)
-                    squares += value * value
-                block = jnp.dot(
-                    jnp.concatenate(parts, axis=1),
-                    jnp.concatenate([gathered[p, source] for p in order], axis=1),
+            sources = far_first[::-1]
+            split = (n_pieces) * HEAD_DIM
+
+            def source_block(source):
+                return jnp.concatenate(
+                    [stream_ref[source * heads + h] for h in range(heads)], axis=1
+                )
+
+            def product(source, pieces):
+                return jnp.dot(
+                    source_block(source),
+                    jnp.concatenate([gathered[p, source] for p in pieces], axis=1),
                     preferred_element_type=f32,
                 )
-                sums_ref[...] = block if n == 0 else sums_ref[...] + block
+
+            def add_squares(source, squares):
+                for h in range(heads):
+                    value = stream_ref[source * heads + h].astype(f32)
+                    squares += value * value
+                return squares
+
+            squares = jnp.zeros((tokens, HEAD_DIM), f32)
+            for n, source in enumerate(sources[:-1]):
+                stream_arrived(source)
+                squares = add_squares(source, squares)
+                block = product(source, order[:-1])
+                if n == 0:
+                    sums_ref[:, :split] = block
+                else:
+                    sums_ref[:, :split] += block
+            arrived(order[-1], False)
+            block = product(sources[0], order[-1:])
+            for source in sources[1:-1]:
+                block += product(source, order[-1:])
+            sums_ref[:, split:] = block
+            stream_arrived(sources[-1])
+            squares = add_squares(sources[-1], squares)
+            sums_ref[...] += product(sources[-1], order)
             mean = jnp.sum(squares, axis=1, keepdims=True) / features
             scale = lax.rsqrt(mean + norm_eps)
 

time: 27.5 us -> 28 us (1.018)
  Pallas kernels: 26.7 us -> 27 us
where the time goes in v3:
time: 28 us; the launch traced here: 27.7 us
  Pallas kernels  27 us (96%)
  between operations  0.64 us (2%)
    pallas_call x1, Pallas kernels, sections_call(): pl.pallas_call(functools.partial(sections_kernel, n_dp, n_tensor), out_sh...  25.4 us
    pallas_call x1, Pallas kernels, write_call(): pl.pallas_call(write_kernel, in_specs=[pl.BlockSpec(memory_space=pltpu.VM...  1.62 us

profile of v3, /device:TPU:1, one launch (start us, length us, event | category | flops | bytes accessed | tf_op | source)
XLA Modules:
  0.0 27.7 jit_solution(7759025444501301736)
XLA Ops:
  0.6 25.4 %shard_map.153 = (f32[1,384,384]{2,1,0:T(8,128)S(1)}, f32[1,384,384]{2,1,0:T(8,128)S(1)}, f32[1,384,384]{2,1,0:T(8,128)S(1)}, f32[1,384,128]{2,1,0:T(8,128)S(1)}...) custom-call(bf16[192,1536]{1,0:T(8,128)(2,1)} %x_hbm.1, s32[1,192]{1,0:T(1,128)} %seg_hbm.1, ...), custom_call_target="tpu_custom_call" | custom-call | tf_op jit(solution)/shard_map/pallas_call | solution.py:492
  26.1 1.6 %shard_map.154 = (f32[1,384,384]{2,1,0:T(8,128)}, f32[1,384,384]{2,1,0:T(8,128)}, f32[1,384,384]{2,1,0:T(8,128)}, f32[1,384,128]{2,1,0:T(8,128)}, f32[1,384,128]...) custom-call(f32[1,384,384]{2,1,0:T(8,128)S(1)} %get-tuple-element.21.refs_0_, ...), custom_call_target="tpu_custom_call" | custom-call | tf_op jit(solution)/shard_map/pallas_call | solution.py:52

commit v4 on v3

--- a/solution.py
+++ b/solution.py
@@ -32,16 +32,9 @@
 def write_kernel(*refs):
     count = (len(refs) - 1) // 2
     sems = refs[-1]
-    copies = []
-    for i in range(count):
-        source, target = refs[i], refs[count + i]
-        rows = source.shape[-2]
-        step = rows // 3 if rows % 24 == 0 and source.dtype == jnp.float32 else rows
-        for n in range(rows // step):
-            at = (Ellipsis, pl.ds(n * step, step), slice(None))
-            copies.append(
-                pltpu.make_async_copy(source.at[at], target.at[at], sems.at[i, n])
-            )
+    copies = [
+        pltpu.make_async_copy(refs[i], refs[count + i], sems.at[i]) for i in range(count)
+    ]
     for copy in copies:
         copy.start()
     for copy in copies:
@@ -51,10 +44,10 @@
 def write_call(arrays):
     return pl.pallas_call(
         write_kernel,
-        in_specs=[pl.BlockSpec(memory_space=pltpu.VMEM)] * len(arrays),
+        in_specs=[pl.BlockSpec(memory_space=pl.ANY)] * len(arrays),
         out_specs=[pl.BlockSpec(memory_space=pl.ANY)] * len(arrays),
         out_shape=[jax.ShapeDtypeStruct(a.shape, a.dtype) for a in arrays],
-        scratch_shapes=[pltpu.SemaphoreType.DMA((len(arrays), 3))],
+        scratch_shapes=[pltpu.SemaphoreType.DMA((len(arrays),))],
     )(*[pltpu.with_memory_space_constraint(a, pltpu.VMEM) for a in arrays])
 
 
@@ -188,7 +181,7 @@
     def update_k(i, carry):
         at = pl.ds(pl.multiple_of(i * step_rows, step_rows), step_rows)
         new = adamw(k_ref[0, at], k_ref[1, at], k_ref[2, at], k_ref[3, at])
-        nmk[0, at], nek[0, at], nsk[0, at] = new
+        k_ref[0, at], k_ref[1, at], k_ref[2, at] = new
         gathered[0, dp, at] = new[0].astype(bf16)
         return carry
 
@@ -198,7 +191,7 @@
         def step(i, carry):
             at = pl.ds(pl.multiple_of(i * step_rows, step_rows), step_rows)
             new = adamw(*[q_ref[n, at, columns] for n in range(4)])
-            nmq[0, at, columns], neq[0, at, columns], nsq[0, at, columns] = new
+            q_ref[0, at, columns], q_ref[1, at, columns], q_ref[2, at, columns] = new
             gathered[1 + head, dp, at] = new[0].astype(bf16)
             return carry
 
@@ -328,7 +321,7 @@
     lax.fori_loop(0, rows // step_rows, update_k, 0)
     pl.semaphore_wait(barrier, len(near) + 1 + n_tensor - (n_tensor == 4))
 
-    direct_pieces = (0, 1)
+    direct_pieces = (0, n_pieces - 1)
 
     @pl.when(pipe == 0)
     def _():
@@ -347,6 +340,12 @@
         def _():
             send(1 + head, 1 + head in direct_pieces)
 
+    keeps = [
+        pltpu.make_async_copy(ref.at[n], out.at[0], load_sem.at[4 * m + n])
+        for m, (ref, outs) in enumerate(((k_ref, (nmk, nek, nsk)), (q_ref, (nmq, neq, nsq))))
+        for n, out in enumerate(outs)
+    ]
+    start(keeps)
     load_x.wait()
     load_seg.wait()
 
@@ -359,15 +358,17 @@
         block = jnp.dot(normed_ref[...], weights(0), preferred_element_type=f32)
         kv_ref[slot] = key_or_value(block, holds_key)
         exchange.start()
+        for p in range(1, n_pieces):
+            if p not in direct_pieces:
+                relay(p)
         pl.semaphore_signal(
             go_sem, inc=1, device_id=(dp, 1, tensor), device_id_type=MESH
         )
-        for head in range(heads):
+        for n in range(heads):
+            head = (n + heads - 1) % heads
             arrived(1 + head, 1 + head in direct_pieces)
             project(head)
-            if head == 0:
-                for p in range(2, n_pieces):
-                    relay(p)
+            if n == 0:
                 exchange.wait()
             columns = pl.ds(
                 pl.multiple_of((tensor * heads + head) * HEAD_DIM, HEAD_DIM), HEAD_DIM
@@ -382,6 +383,8 @@
         for head in range(heads):
             for t in range(n_tensor):
                 stream_copy(head, t).wait_send()
+        for keep in keeps:
+            keep.wait()
 
     @pl.when(pipe == 1)
     def _():
@@ -476,6 +479,8 @@
             ).astype(bf16)
         for p in order:
             all_sent(p, False)
+        for keep in keeps:
+            keep.wait()
 
 
 def sections_call(n_dp, n_tensor, stream, segments, q_arrays, kv_arrays):
@@ -495,7 +500,7 @@
         + [pltpu.VMEM((1, rows, kv_cols), f32)] * 3
         + [pltpu.VMEM((tokens, q_cols), bf16)],
         in_specs=[anywhere] * 10,
-        out_specs=[vmem] * 7,
+        out_specs=[anywhere] * 6 + [vmem],
         scratch_shapes=[
             pltpu.VMEM((tokens, features), bf16),
             pltpu.VMEM(segments.shape, jnp.int32),

time: 28 us -> 27.8 us (level)
  no operation moved by 1% of the time
where the time goes in v4:
time: 27.8 us; the launch traced here: 27.7 us
  Pallas kernels  27 us (97%)
  between operations  0.64 us (2%)
    pallas_call x1, Pallas kernels, sections_call(): pl.pallas_call(functools.partial(sections_kernel, n_dp, n_tensor), out_sh...  25.5 us
    pallas_call x1, Pallas kernels, write_call(): pl.pallas_call(write_kernel, in_specs=[pl.BlockSpec(memory_space=pl.ANY)]...  1.5 us

profile of v4, /device:TPU:1, one launch (start us, length us, event | category | flops | bytes accessed | tf_op | source)
XLA Modules:
  0.0 27.7 jit_solution(2276317407785857578)
XLA Ops:
  0.6 25.5 %shard_map.153 = (f32[1,384,384]{2,1,0:T(8,128)S(1)}, f32[1,384,384]{2,1,0:T(8,128)S(1)}, f32[1,384,384]{2,1,0:T(8,128)S(1)}, f32[1,384,128]{2,1,0:T(8,128)S(1)}...) custom-call(bf16[192,1536]{1,0:T(8,128)(2,1)} %x_hbm.1, s32[1,192]{1,0:T(1,128)} %seg_hbm.1, ...), custom_call_target="tpu_custom_call" | custom-call | tf_op jit(solution)/shard_map/pallas_call | solution.py:497
  26.2 1.5 %shard_map.154 = (f32[1,384,384]{2,1,0:T(8,128)}, f32[1,384,384]{2,1,0:T(8,128)}, f32[1,384,384]{2,1,0:T(8,128)}, f32[1,384,128]{2,1,0:T(8,128)}, f32[1,384,128]...) custom-call(f32[1,384,384]{2,1,0:T(8,128)S(1)} %get-tuple-element.21.refs_0_, ...), custom_call_target="tpu_custom_call" | custom-call | tf_op jit(solution)/shard_map/pallas_call | solution.py:45

commit v5 on v4

--- a/solution.py
+++ b/solution.py
@@ -44,7 +44,7 @@
 def write_call(arrays):
     return pl.pallas_call(
         write_kernel,
-        in_specs=[pl.BlockSpec(memory_space=pl.ANY)] * len(arrays),
+        in_specs=[pl.BlockSpec(memory_space=pltpu.VMEM)] * len(arrays),
         out_specs=[pl.BlockSpec(memory_space=pl.ANY)] * len(arrays),
         out_shape=[jax.ShapeDtypeStruct(a.shape, a.dtype) for a in arrays],
         scratch_shapes=[pltpu.SemaphoreType.DMA((len(arrays),))],
@@ -89,7 +89,6 @@
     send_sem,
     recv_sem,
     pair_sem,
-    stream_send,
     stream_recv,
     go_sem,
 ):
@@ -116,7 +115,7 @@
     blockwise = rows == heads * HEAD_DIM and n_dp == n_tensor
 
     x_side = dp + 1 - 2 * lax.rem(dp, 2)
-    y_side = lax.rem(dp + 2, 4)
+    y_side = lax.rem(dp + 2, n_dp)
 
     barrier = pltpu.get_barrier_semaphore()
     if relayed:
@@ -133,18 +132,14 @@
             barrier, inc=1, device_id=(dp, 1 - pipe, t), device_id_type=MESH
         )
 
-    load_x = pltpu.make_async_copy(x_hbm, x_ref, load_sem.at[8])
-    load_seg = pltpu.make_async_copy(seg_hbm, seg_ref, load_sem.at[9])
-    loads_k = [
-        pltpu.make_async_copy(ref.at[0], k_ref.at[i], load_sem.at[i])
-        for i, ref in enumerate((mk_hbm, ek_hbm, sk_hbm, gk_hbm))
-    ]
-    loads_q = [
-        pltpu.make_async_copy(ref.at[0], q_ref.at[i], load_sem.at[4 + i])
-        for i, ref in enumerate((mq_hbm, eq_hbm, sq_hbm, gq_hbm))
-    ]
-    for load in loads_k + loads_q + [load_x, load_seg]:
-        load.start()
+    load_x = pltpu.make_async_copy(x_hbm, x_ref, load_sem.at[2])
+    load_seg = pltpu.make_async_copy(seg_hbm, seg_ref, load_sem.at[3])
+    for n, ref in enumerate((mk_hbm, ek_hbm, sk_hbm, gk_hbm)):
+        pltpu.make_async_copy(ref.at[0], k_ref.at[n], load_sem.at[0]).start()
+    for n, ref in enumerate((mq_hbm, eq_hbm, sq_hbm, gq_hbm)):
+        pltpu.make_async_copy(ref.at[0], q_ref.at[n], load_sem.at[1]).start()
+    load_x.start()
+    load_seg.start()
 
     def norm(read_block):
         blocks = features // HEAD_DIM
@@ -181,7 +176,7 @@
     def update_k(i, carry):
         at = pl.ds(pl.multiple_of(i * step_rows, step_rows), step_rows)
         new = adamw(k_ref[0, at], k_ref[1, at], k_ref[2, at], k_ref[3, at])
-        k_ref[0, at], k_ref[1, at], k_ref[2, at] = new
+        nmk[0, at], nek[0, at], nsk[0, at] = new
         gathered[0, dp, at] = new[0].astype(bf16)
         return carry
 
@@ -191,7 +186,7 @@
         def step(i, carry):
             at = pl.ds(pl.multiple_of(i * step_rows, step_rows), step_rows)
             new = adamw(*[q_ref[n, at, columns] for n in range(4)])
-            q_ref[0, at, columns], q_ref[1, at, columns], q_ref[2, at, columns] = new
+            nmq[0, at, columns], neq[0, at, columns], nsq[0, at, columns] = new
             gathered[1 + head, dp, at] = new[0].astype(bf16)
             return carry
 
@@ -204,7 +199,7 @@
         return pltpu.make_async_remote_copy(
             src_ref=ref,
             dst_ref=ref,
-            send_sem=send_sem.at[piece, kind],
+            send_sem=send_sem.at[0],
             recv_sem=recv_sem.at[piece, kind],
             device_id=(peer, pipe, tensor),
             device_id_type=MESH,
@@ -212,33 +207,26 @@
 
     def direct_copies(piece):
         own = gathered.at[piece, dp]
-        if relayed:
-            return [
-                copy_to(3 - dp, own, piece, 0),
-                copy_to(x_side, own, piece, 1),
-                copy_to(y_side, own, piece, 2),
-            ]
-        return [copy_to(peer, own, piece, n) for n, peer in enumerate(near)]
+        peers = [3 - dp, x_side, y_side] if relayed else near
+        return [copy_to(peer, own, piece, 2) for peer in peers]
 
     def own_copies(piece, kinds=range(4)):
         peers = (x_side, y_side, x_side, y_side)
         parts = (part_a, part_b, part_b, part_a)
         return [
-            copy_to(peers[n], gathered.at[piece, dp, parts[n]], piece, n) for n in kinds
+            copy_to(peers[n], gathered.at[piece, dp, parts[n]], piece, min(n, 2))
+            for n in kinds
         ]
 
     def relay_copies(piece):
         return [
-            copy_to(y_side, gathered.at[piece, x_side, part_a], piece, 4),
-            copy_to(x_side, gathered.at[piece, y_side, part_b], piece, 5),
+            copy_to(y_side, gathered.at[piece, x_side, part_a], piece, 2),
+            copy_to(x_side, gathered.at[piece, y_side, part_b], piece, 2),
         ]
 
-    def start(copies):
-        for copy in copies:
+    def send(piece, direct):
+        for copy in direct_copies(piece) if direct or not relayed else own_copies(piece):
             copy.start()
-
-    def send(piece, direct):
-        start(direct_copies(piece) if direct or not relayed else own_copies(piece))
 
     def relay(piece):
         if not relayed:
@@ -248,20 +236,12 @@
             passed.start()
 
     def arrived(piece, direct):
-        if direct or not relayed:
-            copies = direct_copies(piece)
-        else:
-            copies = own_copies(piece, (2, 3)) + relay_copies(piece)
-        for copy in copies:
-            copy.wait_recv()
-
-    def all_sent(piece, direct):
-        if direct or not relayed:
-            copies = direct_copies(piece)
-        else:
-            copies = own_copies(piece) + relay_copies(piece)
-        for copy in copies:
-            copy.wait_send()
+        rest = n_dp - 1 if direct or not relayed else n_dp - 2
+        copy_to(x_side, gathered.at[piece, pl.ds(0, rest)], piece, 2).wait_recv()
+
+    def all_sent(count):
+        whole = gathered.at[pl.ds(0, count), pl.ds(0, n_dp - 1)]
+        copy_to(x_side, whole, 0, 2).wait_send()
 
     def weights(piece):
         return gathered[piece].reshape(n_dp * rows, HEAD_DIM)
@@ -308,16 +288,25 @@
         return pltpu.make_async_remote_copy(
             src_ref=first_ref.at[head],
             dst_ref=stream_ref.at[tensor * heads + head],
-            send_sem=stream_send.at[head, to_tensor],
-            recv_sem=stream_recv.at[tensor * heads + head],
+            send_sem=send_sem.at[1],
+            recv_sem=stream_recv.at[tensor],
             device_id=(dp, 1, to_tensor),
             device_id_type=MESH,
         )
 
+    def stream_group(blocks, source):
+        return pltpu.make_async_remote_copy(
+            src_ref=blocks,
+            dst_ref=blocks,
+            send_sem=send_sem.at[1],
+            recv_sem=stream_recv.at[source],
+            device_id=(dp, 1 - pipe, tensor),
+            device_id_type=MESH,
+        )
+
     weight_exchange = pair_block(gathered.at[0, dp], gathered.at[n_pieces, dp])
 
-    for load in loads_k:
-        load.wait()
+    pltpu.make_async_copy(k_ref, k_ref, load_sem.at[0]).wait()
     lax.fori_loop(0, rows // step_rows, update_k, 0)
     pl.semaphore_wait(barrier, len(near) + 1 + n_tensor - (n_tensor == 4))
 
@@ -331,8 +320,7 @@
     def _():
         weight_exchange.start()
 
-    for load in loads_q:
-        load.wait()
+    pltpu.make_async_copy(q_ref, q_ref, load_sem.at[1]).wait()
     for head in range(heads):
         update_q(head)
 
@@ -340,12 +328,6 @@
         def _():
             send(1 + head, 1 + head in direct_pieces)
 
-    keeps = [
-        pltpu.make_async_copy(ref.at[n], out.at[0], load_sem.at[4 * m + n])
-        for m, (ref, outs) in enumerate(((k_ref, (nmk, nek, nsk)), (q_ref, (nmq, neq, nsq))))
-        for n, out in enumerate(outs)
-    ]
-    start(keeps)
     load_x.wait()
     load_seg.wait()
 
@@ -378,13 +360,8 @@
             for t in far_first:
                 stream_copy(head, t).start()
             out_ref[:, head * HEAD_DIM : (head + 1) * HEAD_DIM] = result
-        for p in range(n_pieces):
-            all_sent(p, p in direct_pieces)
-        for head in range(heads):
-            for t in range(n_tensor):
-                stream_copy(head, t).wait_send()
-        for keep in keeps:
-            keep.wait()
+        all_sent(n_pieces)
+        stream_group(stream_ref, 0).wait_send()
 
     @pl.when(pipe == 1)
     def _():
@@ -400,15 +377,8 @@
             arrived(p, False)
 
         def stream_arrived(source):
-            for head in range(heads):
-                pltpu.make_async_remote_copy(
-                    src_ref=first_ref.at[head],
-                    dst_ref=stream_ref.at[source * heads + head],
-                    send_sem=stream_send.at[head, source],
-                    recv_sem=stream_recv.at[source * heads + head],
-                    device_id=(dp, 0, tensor),
-                    device_id_type=MESH,
-                ).wait_recv()
+            blocks = stream_ref.at[pl.ds(source * heads, heads)]
+            stream_group(blocks, source).wait_recv()
 
         if blockwise:
             sources = far_first[::-1]
@@ -477,10 +447,7 @@
             out_ref[:, head * HEAD_DIM : (head + 1) * HEAD_DIM] = (
                 residual + mixed[head * tokens : (head + 1) * tokens]
             ).astype(bf16)
-        for p in order:
-            all_sent(p, False)
-        for keep in keeps:
-            keep.wait()
+        all_sent(n_pieces + 1)
 
 
 def sections_call(n_dp, n_tensor, stream, segments, q_arrays, kv_arrays):
@@ -489,7 +456,6 @@
     kv_cols = kv_arrays[0].shape[2]
     heads = q_cols // HEAD_DIM
     n_pieces = 1 + heads
-    kinds = 6 if n_dp == 4 else n_dp - 1
     bf16 = jnp.bfloat16
     f32 = jnp.float32
     vmem = pl.BlockSpec(memory_space=pltpu.VMEM)
@@ -500,13 +466,13 @@
         + [pltpu.VMEM((1, rows, kv_cols), f32)] * 3
         + [pltpu.VMEM((tokens, q_cols), bf16)],
         in_specs=[anywhere] * 10,
-        out_specs=[anywhere] * 6 + [vmem],
+        out_specs=[vmem] * 7,
         scratch_shapes=[
             pltpu.VMEM((tokens, features), bf16),
             pltpu.VMEM(segments.shape, jnp.int32),
             pltpu.VMEM((4, rows, q_cols), f32),
             pltpu.VMEM((4, rows, kv_cols), f32),
-            pltpu.SemaphoreType.DMA((10,)),
+            pltpu.SemaphoreType.DMA((4,)),
             pltpu.VMEM((n_pieces + 1, n_dp, rows, HEAD_DIM), bf16),
             pltpu.VMEM((tokens, features), bf16),
             pltpu.VMEM((tokens, HEAD_DIM), jnp.float32),
@@ -517,11 +483,10 @@
             pltpu.VMEM((tokens, (n_pieces + 1) * HEAD_DIM), f32),
             pltpu.VMEM((heads, tokens, HEAD_DIM), bf16),
             pltpu.VMEM((n_tensor * heads, tokens, HEAD_DIM), bf16),
-            pltpu.SemaphoreType.DMA((n_pieces + 1, kinds)),
-            pltpu.SemaphoreType.DMA((n_pieces + 1, kinds)),
             pltpu.SemaphoreType.DMA((2,)),
-            pltpu.SemaphoreType.DMA((heads, n_tensor)),
-            pltpu.SemaphoreType.DMA((n_tensor * heads,)),
+            pltpu.SemaphoreType.DMA((n_pieces + 1, 3)),
+            pltpu.SemaphoreType.DMA((2,)),
+            pltpu.SemaphoreType.DMA((n_tensor,)),
             pltpu.SemaphoreType.REGULAR,
         ],
         compiler_params=pltpu.CompilerParams(collective_id=0, has_side_effects=True),

time: 27.8 us -> 27.1 us (0.975)
  Pallas kernels: 27 us -> 26.3 us
    pallas_call x1, Pallas kernels: 25.5 us -> 24.8 us  [sections_call(): pl.pallas_call(functools.partial(sections_kernel, n_dp, n_tensor), out_sh...]
where the time goes in v5:
time: 27.1 us; the launch traced here: 27 us
  Pallas kernels  26.3 us (97%)
  between operations  0.64 us (2%)
    pallas_call x1, Pallas kernels, sections_call(): pl.pallas_call(functools.partial(sections_kernel, n_dp, n_tensor), out_sh...  24.8 us
    pallas_call x1, Pallas kernels, write_call(): pl.pallas_call(write_kernel, in_specs=[pl.BlockSpec(memory_space=pltpu.VM...  1.5 us

profile of v5, /device:TPU:1, one launch (start us, length us, event | category | flops | bytes accessed | tf_op | source)
XLA Modules:
  0.0 27.0 jit_solution(3260811754001464966)
XLA Ops:
  0.6 24.8 %shard_map.153 = (f32[1,384,384]{2,1,0:T(8,128)S(1)}, f32[1,384,384]{2,1,0:T(8,128)S(1)}, f32[1,384,384]{2,1,0:T(8,128)S(1)}, f32[1,384,128]{2,1,0:T(8,128)S(1)}...) custom-call(bf16[192,1536]{1,0:T(8,128)(2,1)} %x_hbm.1, s32[1,192]{1,0:T(1,128)} %seg_hbm.1, ...), custom_call_target="tpu_custom_call" | custom-call | tf_op jit(solution)/shard_map/pallas_call | solution.py:463
  25.5 1.5 %shard_map.154 = (f32[1,384,384]{2,1,0:T(8,128)}, f32[1,384,384]{2,1,0:T(8,128)}, f32[1,384,384]{2,1,0:T(8,128)}, f32[1,384,128]{2,1,0:T(8,128)}, f32[1,384,128]...) custom-call(f32[1,384,384]{2,1,0:T(8,128)S(1)} %get-tuple-element.21.refs_0_, ...), custom_call_target="tpu_custom_call" | custom-call | tf_op jit(solution)/shard_map/pallas_call | solution.py:45

commit v6 on v5

--- a/solution.py
+++ b/solution.py
@@ -86,10 +86,12 @@
     sums_ref,
     first_ref,
     stream_ref,
+    lent_ref,
     send_sem,
     recv_sem,
     pair_sem,
     stream_recv,
+    lent_sem,
     go_sem,
 ):
     dp = lax.axis_index("dp")
@@ -112,6 +114,7 @@
         far_first = [3 - tensor, pair, tensor + 1 - 2 * lax.rem(tensor, 2), tensor]
     else:
         far_first = [lax.rem(tensor + off, n_tensor) for off in range(n_tensor)]
+    lent = (2, 3) if n_dp == 4 and heads == 3 else ()
     blockwise = rows == heads * HEAD_DIM and n_dp == n_tensor
 
     x_side = dp + 1 - 2 * lax.rem(dp, 2)
@@ -195,11 +198,11 @@
     part_a = pl.ds(0, half_rows)
     part_b = pl.ds(half_rows, half_rows)
 
-    def copy_to(peer, ref, piece, kind):
+    def copy_to(peer, ref, piece, kind, group=0):
         return pltpu.make_async_remote_copy(
             src_ref=ref,
             dst_ref=ref,
-            send_sem=send_sem.at[0],
+            send_sem=send_sem.at[group],
             recv_sem=recv_sem.at[piece, kind],
             device_id=(peer, pipe, tensor),
             device_id_type=MESH,
@@ -219,9 +222,10 @@
         ]
 
     def relay_copies(piece):
+        group = 2 if piece in lent else 0
         return [
-            copy_to(y_side, gathered.at[piece, x_side, part_a], piece, 2),
-            copy_to(x_side, gathered.at[piece, y_side, part_b], piece, 2),
+            copy_to(y_side, gathered.at[piece, x_side, part_a], piece, 2, group),
+            copy_to(x_side, gathered.at[piece, y_side, part_b], piece, 2, group),
         ]
 
     def send(piece, direct):
@@ -239,9 +243,8 @@
         rest = n_dp - 1 if direct or not relayed else n_dp - 2
         copy_to(x_side, gathered.at[piece, pl.ds(0, rest)], piece, 2).wait_recv()
 
-    def all_sent(count):
-        whole = gathered.at[pl.ds(0, count), pl.ds(0, n_dp - 1)]
-        copy_to(x_side, whole, 0, 2).wait_send()
+    def all_sent(blocks, group):
+        copy_to(x_side, blocks, 0, 2, group).wait_send()
 
     def weights(piece):
         return gathered[piece].reshape(n_dp * rows, HEAD_DIM)
@@ -304,14 +307,45 @@
             device_id_type=MESH,
         )
 
+    def lend(piece):
+        return pltpu.make_async_remote_copy(
+            src_ref=gathered.at[piece, dp],
+            dst_ref=lent_ref.at[lent.index(piece)],
+            send_sem=lent_sem.at[0],
+            recv_sem=lent_sem.at[1],
+            device_id=(dp, 0, tensor),
+            device_id_type=MESH,
+        )
+
+    def lent_group():
+        return pltpu.make_async_remote_copy(
+            src_ref=lent_ref,
+            dst_ref=lent_ref,
+            send_sem=lent_sem.at[0],
+            recv_sem=lent_sem.at[1],
+            device_id=(dp, 1 - pipe, tensor),
+            device_id_type=MESH,
+        )
+
+    def send_lent(piece):
+        peers = (x_side, y_side, x_side, y_side)
+        parts = (part_a, part_b, part_b, part_a)
+        for n in range(4):
+            pltpu.make_async_remote_copy(
+                src_ref=lent_ref.at[lent.index(piece), parts[n]],
+                dst_ref=gathered.at[piece, dp, parts[n]],
+                send_sem=send_sem.at[2],
+                recv_sem=recv_sem.at[piece, min(n, 2)],
+                device_id=(peers[n], 1, tensor),
+                device_id_type=MESH,
+            ).start()
+
     weight_exchange = pair_block(gathered.at[0, dp], gathered.at[n_pieces, dp])
 
     pltpu.make_async_copy(k_ref, k_ref, load_sem.at[0]).wait()
     lax.fori_loop(0, rows // step_rows, update_k, 0)
     pl.semaphore_wait(barrier, len(near) + 1 + n_tensor - (n_tensor == 4))
 
-    direct_pieces = (0, n_pieces - 1)
-
     @pl.when(pipe == 0)
     def _():
         send(0, True)
@@ -326,7 +360,13 @@
 
         @pl.when(pipe == 0)
         def _():
-            send(1 + head, 1 + head in direct_pieces)
+            send(1 + head, True)
+
+        if 1 + head in lent:
+
+            @pl.when(pipe == 1)
+            def _():
+                lend(1 + head).start()
 
     load_x.wait()
     load_seg.wait()
@@ -336,21 +376,21 @@
         norm(lambda b: x_ref[:, b * HEAD_DIM : (b + 1) * HEAD_DIM].astype(f32))
         tables()
         exchange = pair_block(kv_ref.at[slot], kv_ref.at[slot])
+        if lent:
+            lent_group().wait_recv()
+            for p in lent:
+                send_lent(p)
         arrived(0, True)
         block = jnp.dot(normed_ref[...], weights(0), preferred_element_type=f32)
         kv_ref[slot] = key_or_value(block, holds_key)
         exchange.start()
-        for p in range(1, n_pieces):
-            if p not in direct_pieces:
-                relay(p)
-        pl.semaphore_signal(
-            go_sem, inc=1, device_id=(dp, 1, tensor), device_id_type=MESH
-        )
-        for n in range(heads):
-            head = (n + heads - 1) % heads
-            arrived(1 + head, 1 + head in direct_pieces)
+        for head in range(heads):
+            arrived(1 + head, True)
             project(head)
-            if n == 0:
+            if head == 0:
+                pl.semaphore_signal(
+                    go_sem, inc=1, device_id=(dp, 1, tensor), device_id_type=MESH
+                )
                 exchange.wait()
             columns = pl.ds(
                 pl.multiple_of((tensor * heads + head) * HEAD_DIM, HEAD_DIM), HEAD_DIM
@@ -360,7 +400,9 @@
             for t in far_first:
                 stream_copy(head, t).start()
             out_ref[:, head * HEAD_DIM : (head + 1) * HEAD_DIM] = result
-        all_sent(n_pieces)
+        all_sent(gathered.at[pl.ds(0, n_pieces), pl.ds(0, n_dp - 1)], 0)
+        if lent:
+            all_sent(gathered.at[0], 2)
         stream_group(stream_ref, 0).wait_send()
 
     @pl.when(pipe == 1)
@@ -368,10 +410,13 @@
         tables()
         weight_exchange.wait()
         order = [0, n_pieces] + list(range(1, n_pieces))
+        if lent:
+            order = [0, n_pieces, 2, 3, 1]
         pl.semaphore_wait(go_sem, 1)
         for p in order:
-            send(p, False)
-        for p in order:
+            if p not in lent:
+                send(p, False)
+        for p in [0, 2, n_pieces, 3, 1] if lent else order:
             relay(p)
         for p in order[:-1] if blockwise else order:
             arrived(p, False)
@@ -438,7 +483,7 @@
         kv_ref[slot] = key_or_value(projected(0), holds_key)
         kv_ref[1 - slot] = key_or_value(projected(1), jnp.logical_not(holds_key))
         queries = [
-            rope(projected(2 + head), cos_ref[...], sin_ref[...]).astype(bf16)
+            rope(projected(order.index(1 + head)), cos_ref[...], sin_ref[...]).astype(bf16)
             for head in range(heads)
         ]
         mixed = mix(jnp.concatenate(queries, axis=0))
@@ -447,7 +492,11 @@
             out_ref[:, head * HEAD_DIM : (head + 1) * HEAD_DIM] = (
                 residual + mixed[head * tokens : (head + 1) * tokens]
             ).astype(bf16)
-        all_sent(n_pieces + 1)
+        rest = n_pieces + 1 - len(lent)
+        all_sent(gathered.at[pl.ds(0, rest), pl.ds(0, n_dp - 1)], 0)
+        if lent:
+            all_sent(gathered.at[0, pl.ds(0, len(lent))], 2)
+            lent_group().wait_send()
 
 
 def sections_call(n_dp, n_tensor, stream, segments, q_arrays, kv_arrays):
@@ -483,10 +532,12 @@
             pltpu.VMEM((tokens, (n_pieces + 1) * HEAD_DIM), f32),
             pltpu.VMEM((heads, tokens, HEAD_DIM), bf16),
             pltpu.VMEM((n_tensor * heads, tokens, HEAD_DIM), bf16),
-            pltpu.SemaphoreType.DMA((2,)),
+            pltpu.VMEM((2, rows, HEAD_DIM), bf16),
+            pltpu.SemaphoreType.DMA((3,)),
             pltpu.SemaphoreType.DMA((n_pieces + 1, 3)),
             pltpu.SemaphoreType.DMA((2,)),
             pltpu.SemaphoreType.DMA((n_tensor,)),
+            pltpu.SemaphoreType.DMA((2,)),
             pltpu.SemaphoreType.REGULAR,
         ],
         compiler_params=pltpu.CompilerParams(collective_id=0, has_side_effects=True),

time: 27.1 us -> 27.3 us (level)
  no operation moved by 1% of the time
where the time goes in v6:
time: 27.3 us; the launch traced here: 27.2 us
  Pallas kernels  26.5 us (97%)
  between operations  0.64 us (2%)
    pallas_call x1, Pallas kernels, sections_call(): pl.pallas_call(functools.partial(sections_kernel, n_dp, n_tensor), out_sh...  25 us
    pallas_call x1, Pallas kernels, write_call(): pl.pallas_call(write_kernel, in_specs=[pl.BlockSpec(memory_space=pltpu.VM...  1.5 us

profile of v6, /device:TPU:1, one launch (start us, length us, event | category | flops | bytes accessed | tf_op | source)
XLA Modules:
  0.0 27.2 jit_solution(1366134208662009606)
XLA Ops:
  0.6 25.0 %shard_map.153 = (f32[1,384,384]{2,1,0:T(8,128)S(1)}, f32[1,384,384]{2,1,0:T(8,128)S(1)}, f32[1,384,384]{2,1,0:T(8,128)S(1)}, f32[1,384,128]{2,1,0:T(8,128)S(1)}...) custom-call(bf16[192,1536]{1,0:T(8,128)(2,1)} %x_hbm.1, s32[1,192]{1,0:T(1,128)} %seg_hbm.1, ...), custom_call_target="tpu_custom_call" | custom-call | tf_op jit(solution)/shard_map/pallas_call | solution.py:512
  25.7 1.5 %shard_map.154 = (f32[1,384,384]{2,1,0:T(8,128)}, f32[1,384,384]{2,1,0:T(8,128)}, f32[1,384,384]{2,1,0:T(8,128)}, f32[1,384,128]{2,1,0:T(8,128)}, f32[1,384,128]...) custom-call(f32[1,384,384]{2,1,0:T(8,128)S(1)} %get-tuple-element.21.refs_0_, ...), custom_call_target="tpu_custom_call" | custom-call | tf_op jit(solution)/shard_map/pallas_call | solution.py:45

commit v7 on v6

--- a/solution.py
+++ b/solution.py
@@ -313,7 +313,7 @@
             dst_ref=lent_ref.at[lent.index(piece)],
             send_sem=lent_sem.at[0],
             recv_sem=lent_sem.at[1],
-            device_id=(dp, 0, tensor),
+            device_id=(dp, 1 - pipe, tensor),
             device_id_type=MESH,
         )
 
@@ -340,6 +340,17 @@
                 device_id_type=MESH,
             ).start()
 
+    def send_lent_direct(piece):
+        for peer in (3 - dp, x_side, y_side):
+            pltpu.make_async_remote_copy(
+                src_ref=lent_ref.at[lent.index(piece)],
+                dst_ref=gathered.at[piece, dp],
+                send_sem=send_sem.at[1],
+                recv_sem=recv_sem.at[piece, 2],
+                device_id=(peer, 0, tensor),
+                device_id_type=MESH,
+            ).start()
+
     weight_exchange = pair_block(gathered.at[0, dp], gathered.at[n_pieces, dp])
 
     pltpu.make_async_copy(k_ref, k_ref, load_sem.at[0]).wait()
@@ -358,15 +369,13 @@
     for head in range(heads):
         update_q(head)
 
-        @pl.when(pipe == 0)
-        def _():
-            send(1 + head, True)
-
         if 1 + head in lent:
-
-            @pl.when(pipe == 1)
+            lend(1 + head).start()
+        else:
+
+            @pl.when(pipe == 0)
             def _():
-                lend(1 + head).start()
+                send(1 + head, True)
 
     load_x.wait()
     load_seg.wait()
@@ -388,9 +397,10 @@
             arrived(1 + head, True)
             project(head)
             if head == 0:
-                pl.semaphore_signal(
-                    go_sem, inc=1, device_id=(dp, 1, tensor), device_id_type=MESH
-                )
+                if not lent:
+                    pl.semaphore_signal(
+                        go_sem, inc=1, device_id=(dp, 1, tensor), device_id_type=MESH
+                    )
                 exchange.wait()
             columns = pl.ds(
                 pl.multiple_of((tensor * heads + head) * HEAD_DIM, HEAD_DIM), HEAD_DIM
@@ -400,23 +410,29 @@
             for t in far_first:
                 stream_copy(head, t).start()
             out_ref[:, head * HEAD_DIM : (head + 1) * HEAD_DIM] = result
-        all_sent(gathered.at[pl.ds(0, n_pieces), pl.ds(0, n_dp - 1)], 0)
+        all_sent(gathered.at[pl.ds(0, n_pieces - len(lent)), pl.ds(0, n_dp - 1)], 0)
         if lent:
             all_sent(gathered.at[0], 2)
+            lent_group().wait_send()
         stream_group(stream_ref, 0).wait_send()
 
     @pl.when(pipe == 1)
     def _():
-        tables()
+        if lent:
+            lent_group().wait_recv()
+            for p in lent:
+                send_lent_direct(p)
+        else:
+            pl.semaphore_wait(go_sem, 1)
         weight_exchange.wait()
         order = [0, n_pieces] + list(range(1, n_pieces))
         if lent:
             order = [0, n_pieces, 2, 3, 1]
-        pl.semaphore_wait(go_sem, 1)
         for p in order:
             if p not in lent:
                 send(p, False)
-        for p in [0, 2, n_pieces, 3, 1] if lent else order:
+        tables()
+        for p in [2, 0, 3, n_pieces, 1] if lent else order:
             relay(p)
         for p in order[:-1] if blockwise else order:
             arrived(p, False)
@@ -496,6 +512,7 @@
         all_sent(gathered.at[pl.ds(0, rest), pl.ds(0, n_dp - 1)], 0)
         if lent:
             all_sent(gathered.at[0, pl.ds(0, len(lent))], 2)
+            all_sent(gathered.at[pl.ds(0, len(lent)), pl.ds(0, n_dp - 1)], 1)
             lent_group().wait_send()
 
 

time: 27.3 us -> 28.2 us (1.033)
  the two profiles are of different devices: /device:TPU:1 before, /device:TPU:3 now
where the time goes in v7:
time: 28.2 us; the launch traced here: 28.1 us
  Pallas kernels  27.4 us (97%)
  between operations  0.64 us (2%)
    pallas_call x1, Pallas kernels, sections_call(): pl.pallas_call(functools.partial(sections_kernel, n_dp, n_tensor), out_sh...  25.9 us
    pallas_call x1, Pallas kernels, write_call(): pl.pallas_call(write_kernel, in_specs=[pl.BlockSpec(memory_space=pltpu.VM...  1.5 us

profile of v7, /device:TPU:3, one launch (start us, length us, event | category | flops | bytes accessed | tf_op | source)
XLA Modules:
  0.0 28.1 jit_solution(2231340018592272955)
XLA Ops:
  0.6 25.9 %shard_map.153 = (f32[1,384,384]{2,1,0:T(8,128)S(1)}, f32[1,384,384]{2,1,0:T(8,128)S(1)}, f32[1,384,384]{2,1,0:T(8,128)S(1)}, f32[1,384,128]{2,1,0:T(8,128)S(1)}...) custom-call(bf16[192,1536]{1,0:T(8,128)(2,1)} %x_hbm.1, s32[1,192]{1,0:T(1,128)} %seg_hbm.1, ...), custom_call_target="tpu_custom_call" | custom-call | tf_op jit(solution)/shard_map/pallas_call | solution.py:529
  26.6 1.5 %shard_map.154 = (f32[1,384,384]{2,1,0:T(8,128)}, f32[1,384,384]{2,1,0:T(8,128)}, f32[1,384,384]{2,1,0:T(8,128)}, f32[1,384,128]{2,1,0:T(8,128)}, f32[1,384,128]...) custom-call(f32[1,384,384]{2,1,0:T(8,128)S(1)} %get-tuple-element.21.refs_0_, ...), custom_call_target="tpu_custom_call" | custom-call | tf_op jit(solution)/shard_map/pallas_call | solution.py:45

commit v8 on v6

--- a/solution.py
+++ b/solution.py
@@ -386,11 +386,12 @@
         exchange.start()
         for head in range(heads):
             arrived(1 + head, True)
-            project(head)
             if head == 0:
                 pl.semaphore_signal(
                     go_sem, inc=1, device_id=(dp, 1, tensor), device_id_type=MESH
                 )
+            project(head)
+            if head == 0:
                 exchange.wait()
             columns = pl.ds(
                 pl.multiple_of((tensor * heads + head) * HEAD_DIM, HEAD_DIM), HEAD_DIM
@@ -418,7 +419,9 @@
                 send(p, False)
         for p in [0, 2, n_pieces, 3, 1] if lent else order:
             relay(p)
-        for p in order[:-1] if blockwise else order:
+        early = order[:-2] if blockwise else order
+        late = order[len(early) :]
+        for p in early:
             arrived(p, False)
 
         def stream_arrived(source):
@@ -427,7 +430,7 @@
 
         if blockwise:
             sources = far_first[::-1]
-            split = (n_pieces) * HEAD_DIM
+            split = len(early) * HEAD_DIM
 
             def source_block(source):
                 return jnp.concatenate(
@@ -448,22 +451,14 @@
                 return squares
 
             squares = jnp.zeros((tokens, HEAD_DIM), f32)
-            for n, source in enumerate(sources[:-1]):
+            for n, source in enumerate(sources):
                 stream_arrived(source)
                 squares = add_squares(source, squares)
-                block = product(source, order[:-1])
+                block = product(source, early)
                 if n == 0:
                     sums_ref[:, :split] = block
                 else:
                     sums_ref[:, :split] += block
-            arrived(order[-1], False)
-            block = product(sources[0], order[-1:])
-            for source in sources[1:-1]:
-                block += product(source, order[-1:])
-            sums_ref[:, split:] = block
-            stream_arrived(sources[-1])
-            squares = add_squares(sources[-1], squares)
-            sums_ref[...] += product(sources[-1], order)
             mean = jnp.sum(squares, axis=1, keepdims=True) / features
             scale = lax.rsqrt(mean + norm_eps)
 
@@ -482,6 +477,13 @@
 
         kv_ref[slot] = key_or_value(projected(0), holds_key)
         kv_ref[1 - slot] = key_or_value(projected(1), jnp.logical_not(holds_key))
+        for p in late:
+            arrived(p, False)
+        if late:
+            block = product(sources[0], late)
+            for source in sources[1:]:
+                block += product(source, late)
+            sums_ref[:, split:] = block
         queries = [
             rope(projected(order.index(1 + head)), cos_ref[...], sin_ref[...]).astype(bf16)
             for head in range(heads)

time: 27.3 us -> 27.7 us (1.015)
  Pallas kernels: 26.5 us -> 26.9 us
    pallas_call x1, Pallas kernels: 25 us -> 25.4 us  [sections_call(): pl.pallas_call(functools.partial(sections_kernel, n_dp, n_tensor), out_sh...]
where the time goes in v8:
time: 27.7 us; the launch traced here: 27.5 us
  Pallas kernels  26.9 us (97%)
  between operations  0.64 us (2%)
    pallas_call x1, Pallas kernels, sections_call(): pl.pallas_call(functools.partial(sections_kernel, n_dp, n_tensor), out_sh...  25.4 us
    pallas_call x1, Pallas kernels, write_call(): pl.pallas_call(write_kernel, in_specs=[pl.BlockSpec(memory_space=pltpu.VM...  1.5 us

profile of v8, /device:TPU:1, one launch (start us, length us, event | category | flops | bytes accessed | tf_op | source)
XLA Modules:
  0.0 27.5 jit_solution(1353305137696023472)
XLA Ops:
  0.6 25.4 %shard_map.153 = (f32[1,384,384]{2,1,0:T(8,128)S(1)}, f32[1,384,384]{2,1,0:T(8,128)S(1)}, f32[1,384,384]{2,1,0:T(8,128)S(1)}, f32[1,384,128]{2,1,0:T(8,128)S(1)}...) custom-call(bf16[192,1536]{1,0:T(8,128)(2,1)} %x_hbm.1, s32[1,192]{1,0:T(1,128)} %seg_hbm.1, ...), custom_call_target="tpu_custom_call" | custom-call | tf_op jit(solution)/shard_map/pallas_call | solution.py:514
  26.0 1.5 %shard_map.154 = (f32[1,384,384]{2,1,0:T(8,128)}, f32[1,384,384]{2,1,0:T(8,128)}, f32[1,384,384]{2,1,0:T(8,128)}, f32[1,384,128]{2,1,0:T(8,128)}, f32[1,384,128]...) custom-call(f32[1,384,384]{2,1,0:T(8,128)S(1)} %get-tuple-element.21.refs_0_, ...), custom_call_target="tpu_custom_call" | custom-call | tf_op jit(solution)/shard_map/pallas_call | solution.py:45
